TPU v7x, 32 devices: a whole 2x2x4 slice. The times are simulated.
32 devices in a mesh: runs: 2 (over y), tiles: 16 (over z, x, core).
Axes of the slice: x: 2, y: 2, z: 4, core: 2. Of those that a mesh axis runs over, the one named last changes fastest.
Arguments:
- features: bfloat16 [32, 256, 2048], P(('runs', 'tiles')), parts along dimension 0, may hold values from -6 to 6
- conv_weight: bfloat16 [2, 2, 9, 256, 256], replicated, may hold values from -0.125 to 0.125
- proj_weight: bfloat16 [2, 256, 128], replicated, may hold values from -0.375 to 0.375
- back_weight: bfloat16 [2, 128, 256], replicated, may hold values from -0.5 to 0.5
- sea_fraction: float32 [16, 2048], P('tiles'), may hold values from 0 to 1
- halo_source: int32 [16, 2, 128], P('tiles'), may hold values from 0 to 256, as said below
- src_cells: int32 [16, 5, 4, 128], P('tiles'), may hold values from 0 to 2047
- dst_cells: int32 [16, 5, 4, 128], P('tiles'), may hold values from 0 to 2048, as said below
Outputs:
- updated: bfloat16 [32, 256, 2048], P(('runs', 'tiles')), parts along dimension 0
There are 2 independent parts, one for each index of `runs`. A program takes and returns all parts, laid end to end along the dimension named above; an argument that names none is the same for every part. Nothing has to cross between parts.
Inputs may be any that keep to these rules, and one draw needn't show every extreme that they name: `halo_source`: the value 2 * 128 means a zero halo cell and occurs on the lower side of the ocean tile of local index 0; the atmosphere tiles at both ends of their arc and the last ocean tile read their own edge row on their outer side. `dst_cells`: entry 2048 marks an unused block; a block is used only if its source tile lies in the other component, and every tile uses all 4 blocks of offset 0.
All inputs are finite; a program needn't handle non-finite values.
Results may differ from a plain program's by a relative error of at most 0.0085.
Values may be sent and summed in bfloat16 or wider, within the bound.
No kernel may reach another device: no remote copies, remote signals or barrier semaphores. Data moves between devices by JAX's collectives and lax.ppermute only.
A program may use at most 64 MiB of HBM per device.

v0:
```python
import jax
import jax.numpy as jnp
from jax import lax
from jax.sharding import PartitionSpec as P


def with_halo(x, sides, width):
    for axis, dim in sides:
        peers, length = (lax.axis_size(axis), x.shape[dim])
        up = [(i, (i + 1) % peers) for i in range(peers)]
        down = [(j, i) for i, j in up]
        last = lax.slice_in_dim(x, length - width, length, axis=dim)
        first = lax.slice_in_dim(x, 0, width, axis=dim)
        before = lax.ppermute(last, axis, up)
        after = lax.ppermute(first, axis, down)
        x = jnp.concatenate([before, x, after], axis=dim)
    return x


def passed_along(value, axis, steps):
    count = lax.axis_size(axis)
    pairs = [(source, (source + steps) % count) for source in range(count)]
    return lax.ppermute(value, axis, pairs)


def residual_block(state, kernel, wet_weight, halo_table):
    channels, cell_count = state.shape
    row_cells = halo_table.shape[1]
    lat_rows = cell_count // row_cells
    activated = jax.nn.gelu(state.astype(jnp.float32), approximate=True).astype(jnp.bfloat16)
    activated = activated.reshape(channels, lat_rows, row_cells)
    boundary = jnp.stack([activated[:, 0, :], activated[:, lat_rows - 1, :]])
    extended = with_halo(boundary, (("tiles", 0),), 1)
    zero_col = jnp.zeros((channels, 1), jnp.bfloat16)
    lower_src = jnp.concatenate([extended[0], activated[:, 0, :], zero_col], axis=1)
    upper_src = jnp.concatenate([extended[3], activated[:, lat_rows - 1, :], zero_col], axis=1)
    lower_row = jnp.take(lower_src, halo_table[0], axis=1)
    upper_row = jnp.take(upper_src, halo_table[1], axis=1)
    padded = jnp.concatenate([lower_row[:, None], activated, upper_row[:, None]], axis=1)
    convolved = jnp.zeros((channels, lat_rows, row_cells), jnp.float32)
    for row_off in range(3):
        for col_off in range(3):
            shifted = jnp.roll(padded[:, row_off : row_off + lat_rows, :], 1 - col_off, axis=2)
            convolved = convolved + jnp.einsum(
                "io,irc->orc",
                kernel[row_off * 3 + col_off],
                shifted,
                preferred_element_type=jnp.float32,
            )
    return (
        state.astype(jnp.float32) + wet_weight[None, :] * convolved.reshape(channels, cell_count)
    ).astype(jnp.bfloat16)


def remap_add(state, project_weight, return_weight, source_table, target_table, half_count):
    channels, cell_count = state.shape
    offset_count = source_table.shape[0]
    reach_slots = offset_count // 2
    projected = jnp.einsum(
        "cn,ck->nk", state, project_weight, preferred_element_type=jnp.float32
    ).astype(jnp.bfloat16)
    outgoing = projected[source_table]
    incoming = []
    for offset_slot in range(offset_count):
        incoming.append(
            passed_along(outgoing[offset_slot], "tiles", half_count + offset_slot - reach_slots)
        )
    received = jnp.stack(incoming)
    coupling = received.shape[-1]
    summed = jnp.zeros((cell_count, coupling), jnp.float32)
    summed = summed.at[target_table.reshape(-1)].add(
        received.reshape(-1, coupling).astype(jnp.float32), mode="drop"
    )
    remapped = summed.astype(jnp.bfloat16)
    returned = jnp.einsum("nk,ko->on", remapped, return_weight, preferred_element_type=jnp.float32)
    return (state.astype(jnp.float32) + returned).astype(jnp.bfloat16)


def on_device(
    features, conv_weight, proj_weight, back_weight, sea_fraction, halo_source, src_cells, dst_cells
):
    tile_total = lax.axis_size("tiles")
    half_count = tile_total // 2
    position = (lax.axis_index("tiles") + half_count // 2) % tile_total
    component = (position >= half_count).astype(jnp.int32)
    wet_weight = jnp.where(component == 1, sea_fraction[0], jnp.float32(1.0))
    kernels = lax.dynamic_index_in_dim(conv_weight, component, 0, keepdims=False)
    project_weight = lax.dynamic_index_in_dim(proj_weight, component, 0, keepdims=False)
    return_weight = lax.dynamic_index_in_dim(back_weight, component, 0, keepdims=False)
    state = features[0]
    state = residual_block(state, kernels[0], wet_weight, halo_source[0])
    state = remap_add(state, project_weight, return_weight, src_cells[0], dst_cells[0], half_count)
    state = residual_block(state, kernels[1], wet_weight, halo_source[0])
    return state[None]


def solution(mesh):
    placed = (
        P(("runs", "tiles"), None, None),
        P(),
        P(),
        P(),
        P("tiles", None),
        P("tiles", None, None),
        P("tiles", None, None, None),
        P("tiles", None, None, None),
    )
    return jax.shard_map(
        on_device,
        mesh=mesh,
        in_specs=placed,
        out_specs=P(("runs", "tiles"), None, None),
        check_vma=False,
    )
```

profile of v0, /device:TPU:0, one launch (start us, length us, event | category | flops | bytes accessed | tf_op | source)
XLA Modules:
  0.0 132.3 jit_solution(9170165621772137968)
XLA Ops:
  0.0 1.5 %copy.9 = f32[1,256,2048]{1,2,0:T(8,128)S(1)} copy(bf16[1,256,2048]{2,1,0:T(8,128)(2,1)} %param.10) | data formatting | bytes 3145728 | tf_op jit(solution)/shard_map/convert_element_type | solution.py:51
  2.8 5.0 %collective-permute-start.1 = (bf16[1,256,128]{1,2,0:T(8,128)(2,1)S(1)}, bf16[1,256,128]{1,2,0:T(8,128)(2,1)S(1)}, u32[]{:S(2)}, u32[]{:S(2)}) collective-permute-start(bf16[1,256,128]{1,2,0:T(8,128)(2,1)S(1)} %get-tuple-element.52), channel_id=1, source_target_pairs={{1,0},{2,1},{3,2},{4,3},{5,4},{6,5},{7,6},{8,7},{9,8},{10,9},{11,1... | collective-permute-start | bytes 196616 | tf_op jit(solution)/shard_map/ppermute | solution.py:15
  8.0 3.6 %fusion.43 = f32[256,2048]{0,1} fusion(bf16[1,256,2048]{2,1,0:T(8,128)(2,1)} %param.10, bf16[2,2,9,256,256]{4,3,2,1,0:T(8,128)(2,1)} %param.11, s32[]{:T(128)S(6)} %select_n.54, s32[]{:T(128)S(6)} %add.180), kind=kOutput, calls=%fused_computation.76 | convolution fusion | flops 273678336 | bytes 3276808
  15.1 1.9 %fusion.38 = (bf16[256,16,128]{0,2,1:T(8,128)(2,1)S(1)}, bf16[256,16,128]{0,2,1:T(8,128)(2,1)S(1)}, bf16[256,16,128]{0,2,1:T(8,128)(2,1)S(1)}, bf16[256,16,128]{...) fusion(bf16[256,1,128]{0,2,1:T(8,128)(2,1)S(1)} %select_bitcast_fusion.3, ...), kind=kLoop, calls=%fused_computation.72 | loop fusion | flops 16777216 | bytes 11632640 | tf_op jit(solution)/shard_map/concatenate | solution.py:39
  17.0 2.7 %fusion.76 = f32[256,2048]{0,1} fusion(bf16[256,2048]{0,1:T(8,128)(2,1)S(1)} %bitcast.240, bf16[2,2,9,256,256]{4,3,2,1,0:T(8,128)(2,1)} %param.11, s32[]{:T(128)S(6)} %select_n.54), kind=kOutput, calls=%fused_computation.142 | convolution fusion | flops 268435456 | bytes 3276804
  26.9 2.7 %fusion.72 = f32[256,2048]{0,1} fusion(bf16[256,2048]{0,1:T(8,128)(2,1)S(1)} %bitcast.242, bf16[2,2,9,256,256]{4,3,2,1,0:T(8,128)(2,1)} %param.11, s32[]{:T(128)S(6)} %select_n.54, s32[]{:T(128)S(6)} %add.181), kind=kOutput, calls=%fused_computation.133 | convolution fusion | flops 268435456 | bytes 3276808
  29.6 2.7 %fusion.75 = f32[256,2048]{0,1} fusion(bf16[256,2048]{0,1:T(8,128)(2,1)S(1)} %bitcast.230, bf16[2,2,9,256,256]{4,3,2,1,0:T(8,128)(2,1)} %param.11, s32[]{:T(128)S(6)} %select_n.54, s32[]{:T(128)S(6)} %add.177), kind=kOutput, calls=%fused_computation.140 | convolution fusion | flops 268435456 | bytes 3276808
  32.3 5.3 %add_add_fusion.1 = f32[256,16,128]{0,2,1:T(8,128)S(1)} fusion(f32[256,16,128]{0,2,1:T(8,128)S(1)} %bitcast.219, f32[256,16,128]{0,2,1:T(8,128)S(1)} %bitcast.221, f32[256,16,128]{0,2,1:T(8,128)S(1)} %bitcast.222, f32[256,16,128]{0,2,1:T(8,128)} %bitcast.225, f32[256,16,128]{0,2,1:T(8,128)} %bitcast.247, f32[256,16,128]{0,2,1:T(8,128)S(1)} %bitcast.218, ...), kind=kLoop, calls=%fused_computation.46 | loop fusion | flops 4194304 | bytes 20971520 | tf_op jit(solution)/shard_map/add | solution.py:44
  37.6 1.8 %copy.12 = f32[1,256,2048]{2,1,0:T(8,128)} copy(f32[1,256,2048]{1,2,0:T(8,128)S(1)} %bitcast.210) | data formatting | bytes 4194304 | tf_op jit(solution)/shard_map/reshape | solution.py:51
  39.4 2.4 %convolution_convert_fusion = bf16[2048,128]{1,0:T(8,128)(2,1)S(1)} fusion(f32[1,256,2048]{2,1,0:T(8,128)} %copy.12, bf16[1,256,2048]{2,1,0:T(8,128)(2,1)} %param.10, f32[2048]{0:T(1024)S(1)} %bitcast.251, bf16[2,256,128]{2,1,0:T(8,128)(2,1)S(1)} %copy-done.5, s32[]{:T(128)S(6)} %select_n.54), kind=kOutput, calls=%fused_computation.20 | convolution fusion | flops 136577024 | bytes 3743748 | tf_op jit(solution)/shard_map/cn,ck->nk/dot_general | solution.py:59
  41.8 5.1 %gather_fusion = bf16[2560,128]{1,0:T(8,128)(2,1)S(1)} fusion(bf16[2048,128]{1,0:T(8,128)(2,1)S(1)} %convolution_convert_fusion, s32[3072]{0:T(1024)S(1)} %pad_clamp_fusion), kind=kCustom, calls=%fused_computation.4 | custom fusion | bytes 1320960 | tf_op jit(solution)/shard_map/gather | solution.py:62
  49.2 1.8 %copy.11 = f32[256,2048]{1,0:T(8,128)} copy(f32[256,2048]{0,1:T(8,128)S(1)} %bitcast.211) | data formatting | bytes 4194304 | tf_op jit(solution)/shard_map/reshape | solution.py:51
  51.1 2.6 %collective-permute-start.5 = (bf16[4,128,128]{2,1,0:T(8,128)(2,1)}, bf16[4,128,128]{2,1,0:T(8,128)(2,1)S(1)}, u32[]{:S(2)}, u32[]{:S(2)}) collective-permute-start(bf16[4,128,128]{2,1,0:T(8,128)(2,1)} %bitcast.56), channel_id=1, source_target_pairs={{0,9},{1,10},{2,11},{3,12},{4,13},{5,14},{6,15},{7,0},{8,1},{9,2},... | collective-permute-start | bytes 393224 | tf_op jit(solution)/shard_map/ppermute | solution.py:23
  55.9 2.1 %collective-permute-start.3 = (bf16[4,128,128]{2,1,0:T(8,128)(2,1)}, bf16[4,128,128]{2,1,0:T(8,128)(2,1)S(1)}, u32[]{:S(2)}, u32[]{:S(2)}) collective-permute-start(bf16[4,128,128]{2,1,0:T(8,128)(2,1)} %bitcast.52), channel_id=1, source_target_pairs={{0,7},{1,8},{2,9},{3,10},{4,11},{5,12},{6,13},{7,14},{8,15},{9,0},... | collective-permute-start | bytes 393224 | tf_op jit(solution)/shard_map/ppermute | solution.py:23
  58.0 18.8 %collective-permute-done.3 = bf16[4,128,128]{2,1,0:T(8,128)(2,1)S(1)} collective-permute-done((bf16[4,128,128]{2,1,0:T(8,128)(2,1)}, bf16[4,128,128]{2,1,0:T(8,128)(2,1)S(1)}, u32[]{:S(2)}, u32[]{:S(2)}) %collective-permute-start.3) | collective-permute-done | bytes 131104 | tf_op jit(solution)/shard_map/ppermute | solution.py:23
  76.9 14.6 %scatter_custom_fusion = f32[2048,128]{1,0:T(8,128)S(1)} fusion(s32[2560]{0:T(1024)} %fusion.81, bf16[2560,128]{1,0:T(8,128)(2,1)S(1)} %bitcast.248, f32[]{:T(128)} %constant.62.clone.1), kind=kCustom, calls=%fused_computation.59 | custom fusion | flops 655360 | bytes 1704448 | tf_op jit(solution)/shard_map/scatter-add | solution.py:71
  91.5 3.7 %fusion.23 = (bf16[256,2048]{1,0:T(8,128)(2,1)S(1)}, bf16[256,2048]{1,0:T(8,128)(2,1)}) fusion(f32[2048,128]{1,0:T(8,128)S(1)} %scatter_custom_fusion, bf16[2,128,256]{2,1,0:T(8,128)(2,1)S(1)} %copy-done, s32[]{:T(128)S(6)} %select_n.54, f32[256,2048]{1,0:T(8,128)} %copy.11, f32[2048]{0:T(1024)S(1)} %bitcast.252, bf16[1,256,2048]{2,1,0:T(8,128)(2,1)S(1)} %copy-done.2), kind=kOutput, calls=%fused_computation.43 | convolution fusion | flops 143392768 | bytes 6365188 | tf_op jit(solution)/shard_map/nk,ko->on/dot_general | solution.py:75
  95.9 4.4 %collective-permute-start.8 = (bf16[1,256,128]{1,2,0:T(8,128)(2,1)S(1)}, bf16[1,256,128]{1,2,0:T(8,128)(2,1)S(1)}, u32[]{:S(2)}, u32[]{:S(2)}) collective-permute-start(bf16[1,256,128]{1,2,0:T(8,128)(2,1)S(1)} %get-tuple-element.39), channel_id=1, source_target_pairs={{1,0},{2,1},{3,2},{4,3},{5,4},{6,5},{7,6},{8,7},{9,8},{10,9},{11,1... | collective-permute-start | bytes 196616 | tf_op jit(solution)/shard_map/ppermute | solution.py:15
  100.3 3.3 %fusion.64 = f32[256,2048]{0,1} fusion(bf16[2,2,9,256,256]{4,3,2,1,0:T(8,128)(2,1)} %param.11, s32[]{:T(128)S(6)} %select_n.54, s32[]{:T(128)S(6)} %add.177, s32[]{:T(128)S(6)} %add.180, bf16[256,2048]{1,0:T(8,128)(2,1)S(1)} %copy-done.3), kind=kOutput, calls=%fused_computation.117 | convolution fusion | flops 273678336 | bytes 3276812
  110.3 1.9 %fusion.32 = (bf16[256,16,128]{0,2,1:T(8,128)(2,1)S(1)}, bf16[256,16,128]{0,2,1:T(8,128)(2,1)S(1)}, bf16[256,16,128]{0,2,1:T(8,128)(2,1)S(1)}, bf16[256,16,128]{...) fusion(bf16[256,1,128]{0,2,1:T(8,128)(2,1)S(1)} %get-tuple-element.70, ...), kind=kLoop, calls=%fused_computation.66 | loop fusion | flops 16777216 | bytes 11632640 | tf_op jit(solution)/shard_map/concatenate | solution.py:39
  117.6 2.7 %fusion.61 = f32[256,2048]{0,1} fusion(bf16[256,2048]{0,1:T(8,128)(2,1)S(1)} %bitcast.236, bf16[2,2,9,256,256]{4,3,2,1,0:T(8,128)(2,1)} %param.11, s32[]{:T(128)S(6)} %select_n.54, s32[]{:T(128)S(6)} %add.177, s32[]{:T(128)S(6)} %add.183), kind=kOutput, calls=%fused_computation.111 | convolution fusion | flops 268435456 | bytes 3276812
  120.2 2.7 %fusion.62 = f32[256,2048]{0,1} fusion(bf16[256,2048]{0,1:T(8,128)(2,1)S(1)} %bitcast.235, bf16[2,2,9,256,256]{4,3,2,1,0:T(8,128)(2,1)} %param.11, s32[]{:T(128)S(6)} %select_n.54, s32[]{:T(128)S(6)} %add.177, s32[]{:T(128)S(6)} %add.182), kind=kOutput, calls=%fused_computation.113 | convolution fusion | flops 268435456 | bytes 3276812
  122.9 6.0 %add_add_fusion = f32[256,16,128]{0,2,1:T(8,128)} fusion(f32[256,16,128]{0,2,1:T(8,128)S(1)} %bitcast.217, f32[256,16,128]{0,2,1:T(8,128)} %bitcast.220, f32[256,16,128]{0,2,1:T(8,128)} %bitcast.224, f32[256,16,128]{0,2,1:T(8,128)S(1)} %bitcast.213, f32[256,16,128]{0,2,1:T(8,128)} %bitcast.246, f32[256,16,128]{0,2,1:T(8,128)S(1)} %bitcast.212, ...), kind=kLoop, calls=%fused_computation.45 | loop fusion | flops 4194304 | bytes 20971520 | tf_op jit(solution)/shard_map/add | solution.py:44
  129.0 2.0 %copy.24 = f32[256,2048]{1,0:T(8,128)S(1)} copy(f32[256,2048]{0,1:T(8,128)} %bitcast.228) | data formatting | bytes 4194304 | tf_op jit(solution)/shard_map/reshape | solution.py:51
  (89 shorter events, 30.5 us)
Async XLA Ops:
  0.0 91.5 %copy-start = (bf16[2,128,256]{2,1,0:T(8,128)(2,1)S(1)}, bf16[2,128,256]{2,1,0:T(8,128)(2,1)}, u32[]{:S(2)}) copy-start(bf16[2,128,256]{2,1,0:T(8,128)(2,1)} %param.13) | copy-start | bytes 393220
  1.5 6.3 %copy-start.13 = (s32[1,2,128]{2,1,0:T(2,128)S(1)}, s32[1,2,128]{2,1,0:T(2,128)}, u32[]{:S(2)}) copy-start(s32[1,2,128]{2,1,0:T(2,128)} %param.15) | copy-start | bytes 3076
  1.5 6.4 %copy-start.6 = (s32[1,5,4,128]{3,2,1,0:T(4,128)S(1)}, s32[1,5,4,128]{3,2,1,0:T(4,128)}, u32[]{:S(2)}) copy-start(s32[1,5,4,128]{3,2,1,0:T(4,128)} %param.16) | copy-start | bytes 30724
  1.5 6.4 %copy-start.7 = (f32[1,2048]{1,0:T(1,128)S(1)}, f32[1,2048]{1,0:T(1,128)}, u32[]{:S(2)}) copy-start(f32[1,2048]{1,0:T(1,128)} %param.14) | copy-start | bytes 24580
  2.2 9.4 %collective-permute-start = (bf16[1,256,128]{1,2,0:T(8,128)(2,1)S(1)}, bf16[1,256,128]{1,2,0:T(8,128)(2,1)S(1)}, u32[]{:S(2)}, u32[]{:S(2)}) collective-permute-start(bf16[1,256,128]{1,2,0:T(8,128)(2,1)S(1)} %get-tuple-element.50), channel_id=1, source_target_pairs={{0,1},{1,2},{2,3},{3,4},{4,5},{5,6},{6,7},{7,8},{8,9},{9,10},{10,1... | collective-permute-start | bytes 196616 | tf_op jit(solution)/shard_map/ppermute | solution.py:14
  2.8 8.9 %collective-permute-start.1 = (bf16[1,256,128]{1,2,0:T(8,128)(2,1)S(1)}, bf16[1,256,128]{1,2,0:T(8,128)(2,1)S(1)}, u32[]{:S(2)}, u32[]{:S(2)}) collective-permute-start(bf16[1,256,128]{1,2,0:T(8,128)(2,1)S(1)} %get-tuple-element.52), channel_id=1, source_target_pairs={{1,0},{2,1},{3,2},{4,3},{5,4},{6,5},{7,6},{8,7},{9,8},{10,9},{11,1... | collective-permute-start | bytes 196616 | tf_op jit(solution)/shard_map/ppermute | solution.py:15
  7.9 4.8 %copy-start.9 = (pred[128]{0:T(512)(128)(4,1)}, pred[128]{0:T(512)(128)(4,1)S(1)}, u32[]{:S(2)}) copy-start(pred[128]{0:T(512)(128)(4,1)S(1)} %get-tuple-element.6) | copy-start | bytes 388
  7.9 5.7 %copy-start.11 = (pred[128]{0:T(512)(128)(4,1)}, pred[128]{0:T(512)(128)(4,1)S(1)}, u32[]{:S(2)}) copy-start(pred[128]{0:T(512)(128)(4,1)S(1)} %get-tuple-element.63) | copy-start | bytes 388
  11.6 3.4 %copy-start.8 = (s32[1024]{0:T(1024)}, s32[1024]{0:T(1024)S(1)}, u32[]{:S(2)}) copy-start(s32[1024]{0:T(1024)S(1)} %pad_clamp_fusion.1) | copy-start | bytes 12292
  37.6 1.9 %copy-start.5 = (bf16[2,256,128]{2,1,0:T(8,128)(2,1)S(1)}, bf16[2,256,128]{2,1,0:T(8,128)(2,1)}, u32[]{:S(2)}) copy-start(bf16[2,256,128]{2,1,0:T(8,128)(2,1)} %param.12) | copy-start | bytes 393220
  47.7 10.3 %collective-permute-start.2 = (bf16[4,128,128]{2,1,0:T(8,128)(2,1)S(1)}, bf16[4,128,128]{2,1,0:T(8,128)(2,1)S(1)}, u32[]{:S(2)}, u32[]{:S(2)}) collective-permute-start(bf16[4,128,128]{2,1,0:T(8,128)(2,1)S(1)} %bitcast.250), channel_id=1, source_target_pairs={{0,6},{1,7},{2,8},{3,9},{4,10},{5,11},{6,12},{7,13},{8,14},{9,15},... | collective-permute-start | bytes 393224 | tf_op jit(solution)/shard_map/ppermute | solution.py:23
  51.1 40.5 %copy-start.2 = (bf16[1,256,2048]{2,1,0:T(8,128)(2,1)S(1)}, bf16[1,256,2048]{2,1,0:T(8,128)(2,1)}, u32[]{:S(2)}) copy-start(bf16[1,256,2048]{2,1,0:T(8,128)(2,1)} %param.10) | copy-start | bytes 3145732
  51.1 25.8 %collective-permute-start.5 = (bf16[4,128,128]{2,1,0:T(8,128)(2,1)}, bf16[4,128,128]{2,1,0:T(8,128)(2,1)S(1)}, u32[]{:S(2)}, u32[]{:S(2)}) collective-permute-start(bf16[4,128,128]{2,1,0:T(8,128)(2,1)} %bitcast.56), channel_id=1, source_target_pairs={{0,9},{1,10},{2,11},{3,12},{4,13},{5,14},{6,15},{7,0},{8,1},{9,2},... | collective-permute-start | bytes 393224 | tf_op jit(solution)/shard_map/ppermute | solution.py:23
  53.6 23.2 %collective-permute-start.6 = (bf16[4,128,128]{2,1,0:T(8,128)(2,1)S(1)}, bf16[4,128,128]{2,1,0:T(8,128)(2,1)S(1)}, u32[]{:S(2)}, u32[]{:S(2)}) collective-permute-start(bf16[4,128,128]{2,1,0:T(8,128)(2,1)S(1)} %bitcast.249), channel_id=1, source_target_pairs={{0,10},{1,11},{2,12},{3,13},{4,14},{5,15},{6,0},{7,1},{8,2},{9,3},... | collective-permute-start | bytes 393224 | tf_op jit(solution)/shard_map/ppermute | solution.py:23
  54.7 22.1 %collective-permute-start.4 = (bf16[4,128,128]{2,1,0:T(8,128)(2,1)}, bf16[4,128,128]{2,1,0:T(8,128)(2,1)S(1)}, u32[]{:S(2)}, u32[]{:S(2)}) collective-permute-start(bf16[4,128,128]{2,1,0:T(8,128)(2,1)} %bitcast.54), channel_id=1, source_target_pairs={{0,8},{1,9},{2,10},{3,11},{4,12},{5,13},{6,14},{7,15},{8,0},{9,1},... | collective-permute-start | bytes 393224 | tf_op jit(solution)/shard_map/ppermute | solution.py:23
  55.9 20.9 %collective-permute-start.3 = (bf16[4,128,128]{2,1,0:T(8,128)(2,1)}, bf16[4,128,128]{2,1,0:T(8,128)(2,1)S(1)}, u32[]{:S(2)}, u32[]{:S(2)}) collective-permute-start(bf16[4,128,128]{2,1,0:T(8,128)(2,1)} %bitcast.52), channel_id=1, source_target_pairs={{0,7},{1,8},{2,9},{3,10},{4,11},{5,12},{6,13},{7,14},{8,15},{9,0},... | collective-permute-start | bytes 393224 | tf_op jit(solution)/shard_map/ppermute | solution.py:23
  95.2 5.1 %copy-start.3 = (bf16[256,2048]{1,0:T(8,128)(2,1)S(1)}, bf16[256,2048]{1,0:T(8,128)(2,1)}, u32[]{:S(2)}) copy-start(bf16[256,2048]{1,0:T(8,128)(2,1)} %get-tuple-element.68) | copy-start | bytes 3145732
  95.8 7.8 %collective-permute-start.7 = (bf16[1,256,128]{1,2,0:T(8,128)(2,1)S(1)}, bf16[1,256,128]{1,2,0:T(8,128)(2,1)S(1)}, u32[]{:S(2)}, u32[]{:S(2)}) collective-permute-start(bf16[1,256,128]{1,2,0:T(8,128)(2,1)S(1)} %get-tuple-element.37), channel_id=1, source_target_pairs={{0,1},{1,2},{2,3},{3,4},{4,5},{5,6},{6,7},{7,8},{8,9},{9,10},{10,1... | collective-permute-start | bytes 196616 | tf_op jit(solution)/shard_map/ppermute | solution.py:14
  95.9 7.8 %collective-permute-start.8 = (bf16[1,256,128]{1,2,0:T(8,128)(2,1)S(1)}, bf16[1,256,128]{1,2,0:T(8,128)(2,1)S(1)}, u32[]{:S(2)}, u32[]{:S(2)}) collective-permute-start(bf16[1,256,128]{1,2,0:T(8,128)(2,1)S(1)} %get-tuple-element.39), channel_id=1, source_target_pairs={{1,0},{2,1},{3,2},{4,3},{5,4},{6,5},{7,6},{8,7},{9,8},{10,9},{11,1... | collective-permute-start | bytes 196616 | tf_op jit(solution)/shard_map/ppermute | solution.py:15
  100.3 5.3 %copy-start.10 = (pred[128]{0:T(512)(128)(4,1)S(1)}, pred[128]{0:T(512)(128)(4,1)}, u32[]{:S(2)}) copy-start(pred[128]{0:T(512)(128)(4,1)} %copy-done.9) | copy-start | bytes 388
  100.3 5.3 %copy-start.12 = (pred[128]{0:T(512)(128)(4,1)S(1)}, pred[128]{0:T(512)(128)(4,1)}, u32[]{:S(2)}) copy-start(pred[128]{0:T(512)(128)(4,1)} %copy-done.11) | copy-start | bytes 388
  129.0 2.0 %copy-start.4 = (bf16[256,2048]{1,0:T(8,128)(2,1)S(1)}, bf16[256,2048]{1,0:T(8,128)(2,1)}, u32[]{:S(2)}) copy-start(bf16[256,2048]{1,0:T(8,128)(2,1)} %get-tuple-element.68) | copy-start | bytes 3145732
  129.0 3.3 %copy-start.1 = (bf16[2,128,256]{2,1,0:T(8,128)(2,1)S(1)}, bf16[2,128,256]{2,1,0:T(8,128)(2,1)}, u32[]{:S(2)}) copy-start(bf16[2,128,256]{2,1,0:T(8,128)(2,1)} %param.13) | copy-start | bytes 393220
where the time goes:
time: 133 us; the launch traced here: 132 us
  matrix products  41.3 us (31%)
  other arithmetic  37.2 us (28%)
  waiting for transfers between devices  18.8 us (14%)
  local copies, waits for them, and re-layouts  17.3 us (13%)
  starting transfers between devices  17.2 us (13%)
    unnamed x18, matrix products  35.2 us
    ppermute x5, waiting for transfers between devices, passed_along(): return lax.ppermute(value, axis, pairs)  18.8 us
    scatter-add x1, other arithmetic, remap_add(): summed.at[target_table.reshape(-1)]  14.6 us
    add x2, other arithmetic, residual_block(): convolved + jnp.einsum('io,irc->orc', kernel[row_off * 3 + col_off], shif...  11.3 us
    ppermute x2, starting transfers between devices, with_halo(): after = lax.ppermute(first, axis, down)  9.45 us
    ppermute x5, starting transfers between devices, passed_along(): return lax.ppermute(value, axis, pairs)  7.13 us
    concatenate x4, other arithmetic, residual_block(): jnp.concatenate([lower_row[:, None], activated, upper_row[:, None]], axis=1)  6.48 us
    reshape x3, local copies, waits for them, and re-layouts, residual_block(): convolved.reshape(channels, cell_count)  5.7 us
  transfers between devices with their start and end apart: 9, of which 1 were waited for; matrix products, arithmetic and copies ran while one was open for 8% of the time, Pallas kernels for 0%

commit v1 on v0

v1 whole, which is shorter than its diff:
```python
import functools

import jax
import jax.numpy as jnp
from jax import lax
from jax.experimental import pallas as pl
from jax.experimental.pallas import tpu as pltpu
from jax.sharding import PartitionSpec as P

F32 = jnp.float32
BF16 = jnp.bfloat16


def dot(a, b):
    return jnp.dot(a, b, preferred_element_type=F32)


def gelu(x):
    return jax.nn.gelu(x, approximate=True)


def column(row, width):
    return jnp.broadcast_to(row, (width, row.shape[1])).T


def wet_column(comp, sea_ref, start, size):
    row = jnp.where(comp == 1, sea_ref[:, start : start + size], F32(1.0))
    col = column(row, size)
    return col


def fill_shifted(xs_ref, row, act):
    width = act.shape[0]
    at = pl.ds(row * width, width)
    xs_ref[0, at, :] = pltpu.roll(act, 1, 0).astype(BF16)
    xs_ref[1, at, :] = act.astype(BF16)
    xs_ref[2, at, :] = pltpu.roll(act, width - 1, 0).astype(BF16)


def conv_rows(xs_ref, w_ref, first, rows, width):
    acc = None
    for a in range(3):
        for b in range(3):
            part = dot(xs_ref[b, pl.ds((first + a) * width, rows * width), :], w_ref[3 * a + b])
            acc = part if acc is None else acc + part
    return acc


def zero_halo(xs_ref, rows, width):
    zeros = jnp.zeros((3, width, xs_ref.shape[2]), BF16)
    xs_ref[:, pl.ds(0, width), :] = zeros
    xs_ref[:, pl.ds((rows + 1) * width, width), :] = zeros


def first_block_kernel(comp_ref, x_ref, w_ref, sea_ref, state_ref, part_ref, xs_ref, *, rows, width, group):
    comp = comp_ref[0]
    channels = x_ref.shape[0]
    zero_halo(xs_ref, rows, width)
    for r in range(rows):
        xt = x_ref[:, r * width : (r + 1) * width].astype(F32).T
        state_ref[pl.ds(r * width, width), :] = xt.astype(BF16)
        fill_shifted(xs_ref, r + 1, gelu(xt))
    for g in range(0, rows, group):
        acc = conv_rows(xs_ref, w_ref, g, group, width)
        for r in range(g, g + group):
            piece = acc[(r - g) * width : (r - g + 1) * width]
            if r == 0:
                part_ref[0] = piece
            elif r == rows - 1:
                part_ref[1] = piece
            else:
                wet = wet_column(comp, sea_ref, r * width, width)
                at = pl.ds(r * width, width)
                wide = jnp.concatenate([wet] * (channels // width), axis=1)
                state_ref[at, :] = (state_ref[at, :].astype(F32) + wide * piece).astype(BF16)


def second_block_kernel(comp_ref, s_ref, w_ref, sea_ref, out_ref, part_ref, xs_ref, *, rows, width, group):
    comp = comp_ref[0]
    channels = s_ref.shape[1]
    zero_halo(xs_ref, rows, width)
    for r in range(rows):
        fill_shifted(xs_ref, r + 1, gelu(s_ref[pl.ds(r * width, width), :].astype(F32)))
    for g in range(0, rows, group):
        acc = conv_rows(xs_ref, w_ref, g, group, width)
        for r in range(g, g + group):
            piece = acc[(r - g) * width : (r - g + 1) * width]
            if r == 0:
                part_ref[0] = piece
            elif r == rows - 1:
                part_ref[1] = piece
            else:
                row = jnp.where(comp == 1, sea_ref[:, r * width : (r + 1) * width], F32(1.0))
                state = s_ref[pl.ds(r * width, width), :].astype(F32).T
                out_ref[:, r * width : (r + 1) * width] = (state + row * piece.T).astype(BF16)


def pick_halo(index_row, received, own):
    width = index_row.shape[1]
    index = column(index_row.astype(F32), width)
    lane = lax.broadcasted_iota(jnp.int32, (width, width), 1).astype(F32)
    first = (index == lane).astype(F32).astype(BF16)
    second = (index == lane + width).astype(F32).astype(BF16)
    return dot(first, received) + dot(second, own)


def halo_conv(halo, w_ref, first_tap):
    width = halo.shape[0]
    return (
        dot(pltpu.roll(halo, 1, 0).astype(BF16), w_ref[first_tap])
        + dot(halo.astype(BF16), w_ref[first_tap + 1])
        + dot(pltpu.roll(halo, width - 1, 0).astype(BF16), w_ref[first_tap + 2])
    )


def project_kernel(
    comp_ref, s_ref, part_ref, lo_ref, hi_ref, table_ref, w_ref, sea_ref, p_ref, src_ref,
    edge_ref, out_ref, *, rows, width, groups,
):
    comp = comp_ref[0]
    channels = s_ref.shape[1]
    cells = rows * width
    coupling = p_ref.shape[1]
    weight = p_ref[...]
    edges = []
    for side in range(2):
        r = 0 if side == 0 else rows - 1
        received = gelu((lo_ref if side == 0 else hi_ref)[...].astype(F32).T).astype(BF16)
        own_state = s_ref[pl.ds(r * width, width), :].astype(F32)
        own = gelu(own_state).astype(BF16)
        halo = pick_halo(table_ref[side : side + 1, :], received, own)
        acc = part_ref[side] + halo_conv(halo, w_ref, 6 * side)
        wet = wet_column(comp, sea_ref, r * width, width)
        wide = jnp.concatenate([wet] * (channels // width), axis=1)
        edge = (own_state + wide * acc).astype(BF16)
        edge_ref[side] = edge
        edges.append(dot(edge, weight).astype(BF16))
    inner = dot(s_ref[pl.ds(width, cells - 2 * width), :], weight).astype(BF16)
    projected = jnp.concatenate([edges[0], inner, edges[1]], axis=0)
    depth = cells // groups
    wide = jnp.concatenate([projected[g * depth : (g + 1) * depth] for g in range(groups)], axis=1)
    lane = lax.broadcasted_iota(jnp.int32, (width, width), 1).astype(F32)
    tiles = depth // width
    for slot in range(out_ref.shape[0]):
        for block in range(out_ref.shape[1] // width):
            row = slot * (out_ref.shape[1] // width) + block
            index = column(src_ref[row : row + 1, :].astype(F32), width)
            group = jnp.floor(index * F32(1.0 / depth))
            inside = index - group * depth
            hot = jnp.concatenate(
                [(inside == lane + k * width).astype(F32).astype(BF16) for k in range(tiles)], axis=1
            )
            taken = dot(hot, wide)
            picked = taken[:, :coupling]
            for g in range(1, groups):
                picked = jnp.where(group == g, taken[:, g * coupling : (g + 1) * coupling], picked)
            out_ref[slot, block * width : (block + 1) * width, :] = picked.astype(BF16)


def land_kernel(comp_ref, *refs, rows, width, groups, slots):
    received = refs[:slots]
    dst_ref, s_ref, edge_ref, b_ref, state_ref, act_ref = refs[slots:]
    cells = rows * width
    coupling = b_ref.shape[0]
    depth = cells // groups
    per_slot = received[0].shape[0] // width
    sub = lax.broadcasted_iota(jnp.int32, (width, width), 0).astype(F32)
    total = None
    for slot in range(slots):
        sides, hots = [], []
        for block in range(per_slot):
            row = slot * per_slot + block
            index = dst_ref[row : row + 1, :].astype(F32)
            group = jnp.floor(index * F32(1.0 / depth))
            inside = index - group * depth
            values = received[slot][block * width : (block + 1) * width, :].astype(F32)
            group_col = column(group, width)
            sides.append(
                jnp.concatenate(
                    [jnp.where(group_col == g, values, 0.0).astype(BF16) for g in range(groups)], axis=1
                )
            )
            hots.append(
                jnp.concatenate(
                    [(inside == sub + k * width).astype(F32).astype(BF16) for k in range(depth // width)], axis=0
                )
            )
        part = dot(jnp.concatenate(hots, axis=1), jnp.concatenate(sides, axis=0))
        total = part if total is None else total + part
    for g in range(groups):
        remapped = total[:, g * coupling : (g + 1) * coupling].astype(BF16)
        returned = dot(remapped, b_ref[...])
        for k in range(depth // width):
            r = g * (depth // width) + k
            if r == 0:
                before = edge_ref[0]
            elif r == rows - 1:
                before = edge_ref[1]
            else:
                before = s_ref[pl.ds(r * width, width), :]
            state = (before.astype(F32) + returned[k * width : (k + 1) * width]).astype(BF16)
            state_ref[pl.ds(r * width, width), :] = state
            if r == 0:
                act_ref[0] = gelu(state.astype(F32)).astype(BF16)
            elif r == rows - 1:
                act_ref[1] = gelu(state.astype(F32)).astype(BF16)


def finish_kernel(comp_ref, out_in_ref, s_ref, part_ref, act_ref, lo_ref, hi_ref, table_ref, w_ref, sea_ref, out_ref):
    del out_in_ref
    comp = comp_ref[0]
    side = pl.program_id(0)

    def one(which, r_ref):
        halo = pick_halo(table_ref[which : which + 1, :], r_ref[...], act_ref[which])
        acc = part_ref[which] + halo_conv(halo, w_ref, 6 * which)
        row = jnp.where(comp == 1, sea_ref[...], F32(1.0))
        state = s_ref[...].astype(F32).T
        out_ref[...] = (state + row * acc.T).astype(BF16)

    pl.when(side == 0)(lambda: one(0, lo_ref))
    pl.when(side == 1)(lambda: one(1, hi_ref))


def whole(shape):
    return pl.BlockSpec(shape, lambda *_: (0,) * len(shape))


def call(kernel, comp, args, specs, out_shape, out_specs, scratch=(), grid=(1,), aliases=None, name=None):
    return pl.pallas_call(
        kernel,
        grid_spec=pltpu.PrefetchScalarGridSpec(
            num_scalar_prefetch=1, grid=grid, in_specs=specs, out_specs=out_specs, scratch_shapes=scratch
        ),
        out_shape=out_shape,
        input_output_aliases=aliases or {},
        name=name,
    )(comp, *args)


def on_device(
    features, conv_weight, proj_weight, back_weight, sea_fraction, halo_source, src_cells, dst_cells
):
    tile_total = lax.axis_size("tiles")
    half = tile_total // 2
    position = (lax.axis_index("tiles") + half // 2) % tile_total
    comp = (position >= half).astype(jnp.int32).reshape(1)
    _, channels, cells = features.shape
    width = halo_source.shape[-1]
    rows = cells // width
    coupling = proj_weight.shape[-1]
    slots = src_cells.shape[1]
    reach = slots // 2
    sent = src_cells.shape[2] * src_cells.shape[3]
    taps = conv_weight.shape[2]

    up = [(t, (t + 1) % tile_total) for t in range(tile_total)]
    down = [(b, a) for a, b in up]

    def remap_pairs(slot):
        pairs = []
        for t in range(tile_total):
            local = (t + half // 2) % tile_total % half
            d = slot - reach
            if 0 <= local - d < half:
                pairs.append(((t - half - d) % tile_total, t))
        return pairs

    def weight_spec(block):
        return pl.BlockSpec((None, None, taps, channels, channels), lambda i, c: (c[0], block, 0, 0, 0))

    def comp_spec(array):
        return pl.BlockSpec((None,) + array.shape[1:], lambda i, c: (c[0],) + (0,) * (array.ndim - 1))

    x = features[0]
    table = halo_source[0]
    src = src_cells[0].reshape(-1, width)
    dst = dst_cells[0].reshape(-1, width)

    lo = lax.ppermute(x[:, cells - width :], "tiles", up)
    hi = lax.ppermute(x[:, :width], "tiles", down)

    part_shape = jax.ShapeDtypeStruct((2, width, channels), F32)
    edge_shape = jax.ShapeDtypeStruct((2, width, channels), BF16)
    state_shape = jax.ShapeDtypeStruct((cells, channels), BF16)
    shifted = pltpu.VMEM((3, (rows + 2) * width, channels), BF16)
    group = 4

    state, part = call(
        functools.partial(first_block_kernel, rows=rows, width=width, group=group),
        comp,
        (x, conv_weight, sea_fraction),
        [whole(x.shape), weight_spec(0), whole(sea_fraction.shape)],
        (state_shape, part_shape),
        (whole(state_shape.shape), whole(part_shape.shape)),
        scratch=[shifted],
        name="block0",
    )
    edge, outgoing = call(
        functools.partial(project_kernel, rows=rows, width=width, groups=4),
        comp,
        (state, part, lo, hi, table, conv_weight, sea_fraction, proj_weight, src),
        [
            whole(state.shape), whole(part.shape), whole(lo.shape), whole(hi.shape), whole(table.shape),
            weight_spec(0), whole(sea_fraction.shape), comp_spec(proj_weight), whole(src.shape),
        ],
        (edge_shape, jax.ShapeDtypeStruct((slots, sent, coupling), BF16)),
        (whole(edge_shape.shape), whole((slots, sent, coupling))),
        name="project",
    )
    received = [lax.ppermute(outgoing[s], "tiles", remap_pairs(s)) for s in range(slots)]
    state, act = call(
        functools.partial(land_kernel, rows=rows, width=width, groups=2, slots=slots),
        comp,
        (*received, dst, state, edge, back_weight),
        [whole(r.shape) for r in received]
        + [whole(dst.shape), whole(state.shape), whole(edge.shape), comp_spec(back_weight)],
        (state_shape, edge_shape),
        (whole(state_shape.shape), whole(edge_shape.shape)),
        name="land",
    )
    lo = lax.ppermute(act[1], "tiles", up)
    hi = lax.ppermute(act[0], "tiles", down)
    out, part = call(
        functools.partial(second_block_kernel, rows=rows, width=width, group=group),
        comp,
        (state, conv_weight, sea_fraction),
        [whole(state.shape), weight_spec(1), whole(sea_fraction.shape)],
        (jax.ShapeDtypeStruct((channels, cells), BF16), part_shape),
        (whole((channels, cells)), whole(part_shape.shape)),
        scratch=[shifted],
        name="block1",
    )
    out = call(
        finish_kernel,
        comp,
        (out, state, part, act, lo, hi, table, conv_weight, sea_fraction),
        [
            pl.BlockSpec(memory_space=pl.ANY),
            pl.BlockSpec((width, channels), lambda i, c: (i * (rows - 1), 0)),
            whole(part.shape), whole(act.shape), whole(lo.shape), whole(hi.shape), whole(table.shape),
            weight_spec(1),
            pl.BlockSpec((1, width), lambda i, c: (0, i * (rows - 1))),
        ],
        jax.ShapeDtypeStruct((channels, cells), BF16),
        pl.BlockSpec((channels, width), lambda i, c: (0, i * (rows - 1))),
        grid=(2,),
        aliases={1: 0},
        name="finish",
    )
    return out[None]


def solution(mesh):
    placed = (
        P(("runs", "tiles"), None, None),
        P(),
        P(),
        P(),
        P("tiles", None),
        P("tiles", None, None),
        P("tiles", None, None, None),
        P("tiles", None, None, None),
    )
    return jax.shard_map(
        on_device,
        mesh=mesh,
        in_specs=placed,
        out_specs=P(("runs", "tiles"), None, None),
        check_vma=False,
    )
```

time: 133 us -> 68.4 us (0.51)
  matrix products: 41.3 us -> 0 us
  other arithmetic: 37.2 us -> 0 us
  Pallas kernels: 0 us -> 25.3 us
  local copies, waits for them, and re-layouts: 17.3 us -> 6.77 us
  waiting for transfers between devices: 18.8 us -> 9.83 us
  starting transfers between devices: 17.2 us -> 25.9 us
    unnamed x18 -> x0, matrix products: 35.2 us -> none
    pallas_call x0 -> x5, Pallas kernels: none -> 25.3 us  [call(): pl.pallas_call(kernel, grid_spec=pltpu.PrefetchScalarGridSpec(num_scalar_...]
    scatter-add x1 -> x0, other arithmetic: 14.6 us -> none  [remap_add(): summed.at[target_table.reshape(-1)]]
    add x2 -> x0, other arithmetic: 11.3 us -> none  [residual_block(): convolved + jnp.einsum('io,irc->orc', kernel[row_off * 3 + col_off], shif...]
    ppermute x9, waiting for transfers between devices: 18.8 us -> 9.83 us  [the longest x5 9.07 us: on_device(): lax.ppermute(outgoing[s], 'tiles', remap_pairs(s))]
    ppermute x9, starting transfers between devices: 17.2 us -> 25.9 us  [the longest x5 16 us: on_device(): lax.ppermute(outgoing[s], 'tiles', remap_pairs(s))]
    gather x5 -> x0, local copies, waits for them, and re-layouts: 8.58 us -> none  [the longest x1 5.07 us: remap_add(): outgoing = projected[source_table]]
    concatenate x10 -> x0, other arithmetic: 7.72 us -> none  [the longest x4 6.48 us: residual_block(): jnp.concatenate([lower_row[:, None], activated, upper_row[:, None]], axis=1)]
  transfers between devices with their start and end apart: 9 -> 9, of which waited for: 1 -> 4; matrix products, arithmetic and copies ran while one was open for 8% -> 3% of each run, Pallas kernels for 0% -> 17%
where the time goes in v1:
time: 68.4 us; the launch traced here: 67.9 us
  starting transfers between devices  25.9 us (38%)
  Pallas kernels  25.3 us (37%)
  waiting for transfers between devices  9.83 us (14%)
  local copies, waits for them, and re-layouts  6.77 us (10%)
    pallas_call x5, Pallas kernels, call(): pl.pallas_call(kernel, grid_spec=pltpu.PrefetchScalarGridSpec(num_scalar_...  25.3 us
    ppermute x5, starting transfers between devices, on_device(): lax.ppermute(outgoing[s], 'tiles', remap_pairs(s))  16 us
    ppermute x5, waiting for transfers between devices, on_device(): lax.ppermute(outgoing[s], 'tiles', remap_pairs(s))  9.07 us
    ppermute x1, starting transfers between devices, on_device(): hi = lax.ppermute(x[:, :width], 'tiles', down)  5.5 us
    ppermute x1, starting transfers between devices, on_device(): hi = lax.ppermute(act[0], 'tiles', down)  4.4 us
    unnamed x20, local copies, waits for them, and re-layouts  1.89 us
  transfers between devices with their start and end apart: 9, of which 4 were waited for; matrix products, arithmetic and copies ran while one was open for 3% of the time, Pallas kernels for 17%

profile of v1, /device:TPU:0, one launch (start us, length us, event | category | flops | bytes accessed | tf_op | source)
XLA Modules:
  0.0 67.9 jit_solution(10396493088159612149)
XLA Ops:
  0.0 0.9 %fusion = (bf16[256,128]{1,0:T(8,128)(2,1)S(1)}, bf16[256,128]{1,0:T(8,128)(2,1)S(1)}) fusion(bf16[256,2048]{1,0:T(8,128)(2,1)} %bitcast.18), kind=kLoop, calls=%fused_computation.7 | loop fusion | bytes 262144 | tf_op jit(solution)/shard_map/slice | solution.py:281
  0.9 5.5 %collective-permute-start.1 = (bf16[256,128]{1,0:T(8,128)(2,1)S(1)}, bf16[256,128]{1,0:T(8,128)(2,1)S(1)}, u32[]{:S(2)}, u32[]{:S(2)}) collective-permute-start(bf16[256,128]{1,0:T(8,128)(2,1)S(1)} %get-tuple-element.21), channel_id=1, source_target_pairs={{1,0},{2,1},{3,2},{4,3},{5,4},{6,5},{7,6},{8,7},{9,8},{10,9},{11,1... | collective-permute-start | bytes 196616 | tf_op jit(solution)/shard_map/ppermute | solution.py:281
  6.4 1.3 %reshape_squeeze.6.src_ref = s32[20,128]{1,0:T(8,128)} reshape(s32[1,5,4,128]{3,2,1,0:T(4,128)} %param.14) | data formatting | bytes 20480 | tf_op jit(solution)/shard_map/reshape;squeeze | solution.py:277
  7.7 5.6 %block0.1 = (bf16[2048,256]{1,0:T(8,128)(2,1)}, f32[2,128,256]{2,1,0:T(8,128)}) custom-call(s32[1]{0:T(128)} %bitcast.comp_ref, bf16[256,2048]{1,0:T(8,128)(2,1)} %bitcast.19, bf16[2,2,9,256,256]{4,3,2,1,0:T(8,128)(2,1)} %w_ref.7, f32[1,2048]{1,0:T(1,128)} %sea_ref.7), custom_call_target="tpu_custom_call" | custom-call | tf_op jit(solution)/shard_map/block0/pallas_call | solution.py:230
  13.4 0.6 copy-done.5
  14.0 5.8 %project.1 = (bf16[2,128,256]{2,1,0:T(8,128)(2,1)}, bf16[5,512,128]{2,1,0:T(8,128)(2,1)}) custom-call(s32[1]{0:T(128)} %bitcast.comp_ref, bf16[2048,256]{1,0:T(8,128)(2,1)} %get-tuple-element.13.s_ref.refs_6_, f32[2,128,256]{2,1,0:T(8,128)} %get-tuple-element.14.part_ref, bf16[256,128]{1,0:T(8,128)(2,1)} %copy-done.6, bf16[256,128]{1,0:T(8,128)(2,1)} %copy-done.5, ...), custom_call_target="tpu_custom_call" | custom-call | tf_op jit(solution)/shard_map/project/pallas_call | solution.py:230
  19.8 1.2 %slice_bitcast_fusion = (bf16[512,128]{1,0:T(8,128)(2,1)S(1)}, bf16[512,128]{1,0:T(8,128)(2,1)S(1)}, bf16[512,128]{1,0:T(8,128)(2,1)S(1)}, bf16[512,128]{1,0:T(8,128)(2,1)S(1)}, bf16[512,128]{1,0:T(8,128)(2,1)S(1)}) fusion(bf16[5,512,128]{2,1,0:T(8,128)(2,1)} %get-tuple-element.15), kind=kLoop, calls=%fused_computation | loop fusion | bytes 1310720 | tf_op jit(solution)/shard_map/squeeze | solution.py:311
  21.0 2.0 %collective-permute-start.6 = (bf16[512,128]{1,0:T(8,128)(2,1)S(1)}, bf16[512,128]{1,0:T(8,128)(2,1)S(1)}, u32[]{:S(2)}, u32[]{:S(2)}) collective-permute-start(bf16[512,128]{1,0:T(8,128)(2,1)S(1)} %get-tuple-element.23), channel_id=1, source_target_pairs={{6,0},{7,1},{8,2},{9,3},{12,6},{13,7},{14,8},{15,9},{0,10},{1,11},... | collective-permute-start | bytes 393224 | tf_op jit(solution)/shard_map/ppermute | solution.py:311
  23.0 3.5 %collective-permute-start.5 = (bf16[512,128]{1,0:T(8,128)(2,1)S(1)}, bf16[512,128]{1,0:T(8,128)(2,1)S(1)}, u32[]{:S(2)}, u32[]{:S(2)}) collective-permute-start(bf16[512,128]{1,0:T(8,128)(2,1)S(1)} %get-tuple-element.24), channel_id=1, source_target_pairs={{7,0},{8,1},{9,2},{10,3},{12,5},{13,6},{14,7},{15,8},{0,9},{1,10},... | collective-permute-start | bytes 393224 | tf_op jit(solution)/shard_map/ppermute | solution.py:311
  26.5 2.7 %collective-permute-start.4 = (bf16[512,128]{1,0:T(8,128)(2,1)S(1)}, bf16[512,128]{1,0:T(8,128)(2,1)S(1)}, u32[]{:S(2)}, u32[]{:S(2)}) collective-permute-start(bf16[512,128]{1,0:T(8,128)(2,1)S(1)} %get-tuple-element.25), channel_id=1, source_target_pairs={{8,0},{9,1},{10,2},{11,3},{12,4},{13,5},{14,6},{15,7},{0,8},{1,9},... | collective-permute-start | bytes 393224 | tf_op jit(solution)/shard_map/ppermute | solution.py:311
  29.2 2.4 %collective-permute-start.3 = (bf16[512,128]{1,0:T(8,128)(2,1)S(1)}, bf16[512,128]{1,0:T(8,128)(2,1)S(1)}, u32[]{:S(2)}, u32[]{:S(2)}) collective-permute-start(bf16[512,128]{1,0:T(8,128)(2,1)S(1)} %get-tuple-element.26), channel_id=1, source_target_pairs={{9,0},{10,1},{11,2},{13,4},{14,5},{15,6},{0,7},{1,8},{2,9},{3,10},... | collective-permute-start | bytes 393224 | tf_op jit(solution)/shard_map/ppermute | solution.py:311
  31.6 5.4 %collective-permute-start.2 = (bf16[512,128]{1,0:T(8,128)(2,1)S(1)}, bf16[512,128]{1,0:T(8,128)(2,1)S(1)}, u32[]{:S(2)}, u32[]{:S(2)}) collective-permute-start(bf16[512,128]{1,0:T(8,128)(2,1)S(1)} %get-tuple-element.27), channel_id=1, source_target_pairs={{10,0},{11,1},{14,4},{15,5},{0,6},{1,7},{2,8},{3,9},{6,12},{7,13},... | collective-permute-start | bytes 393224 | tf_op jit(solution)/shard_map/ppermute | solution.py:311
  37.0 0.6 reshape_squeeze.7.refs_5_
  37.7 5.6 %collective-permute-done.4.refs_2_ = bf16[512,128]{1,0:T(8,128)(2,1)S(1)} collective-permute-done((bf16[512,128]{1,0:T(8,128)(2,1)S(1)}, bf16[512,128]{1,0:T(8,128)(2,1)S(1)}, u32[]{:S(2)}, u32[]{:S(2)}) %collective-permute-start.4) | collective-permute-done | bytes 131104 | tf_op jit(solution)/shard_map/ppermute | solution.py:311
  43.3 1.2 %collective-permute-done.3.refs_1_ = bf16[512,128]{1,0:T(8,128)(2,1)S(1)} collective-permute-done((bf16[512,128]{1,0:T(8,128)(2,1)S(1)}, bf16[512,128]{1,0:T(8,128)(2,1)S(1)}, u32[]{:S(2)}, u32[]{:S(2)}) %collective-permute-start.3) | collective-permute-done | bytes 131104 | tf_op jit(solution)/shard_map/ppermute | solution.py:311
  44.5 2.2 %collective-permute-done.2.refs_0_ = bf16[512,128]{1,0:T(8,128)(2,1)S(1)} collective-permute-done((bf16[512,128]{1,0:T(8,128)(2,1)S(1)}, bf16[512,128]{1,0:T(8,128)(2,1)S(1)}, u32[]{:S(2)}, u32[]{:S(2)}) %collective-permute-start.2) | collective-permute-done | bytes 131104 | tf_op jit(solution)/shard_map/ppermute | solution.py:311
  46.8 0.6 copy-done.4
  47.4 5.0 %land.1 = (bf16[2048,256]{1,0:T(8,128)(2,1)}, bf16[2,128,256]{2,1,0:T(8,128)(2,1)}) custom-call(s32[1]{0:T(128)} %bitcast.comp_ref, bf16[512,128]{1,0:T(8,128)(2,1)} %copy-done.4, bf16[512,128]{1,0:T(8,128)(2,1)} %copy-done.3, bf16[512,128]{1,0:T(8,128)(2,1)} %copy-done.2, bf16[512,128]{1,0:T(8,128)(2,1)} %copy-done.1, bf16[512,128]{1,0:T(8,128)(2,1)} %copy-done, ...), custom_call_target="tpu_custom_call" | custom-call | tf_op jit(solution)/shard_map/land/pallas_call | solution.py:230
  52.4 0.9 %slice_bitcast_fusion.5 = (bf16[128,256]{1,0:T(8,128)(2,1)S(1)}, bf16[128,256]{1,0:T(8,128)(2,1)S(1)}) fusion(bf16[2,128,256]{2,1,0:T(8,128)(2,1)} %get-tuple-element.20.act_ref), kind=kLoop, calls=%fused_computation.5 | loop fusion | bytes 262144 | tf_op jit(solution)/shard_map/squeeze | solution.py:323
  53.3 4.4 %collective-permute-start.8 = (bf16[128,256]{1,0:T(8,128)(2,1)S(1)}, bf16[128,256]{1,0:T(8,128)(2,1)S(1)}, u32[]{:S(2)}, u32[]{:S(2)}) collective-permute-start(bf16[128,256]{1,0:T(8,128)(2,1)S(1)} %get-tuple-element.28), channel_id=1, source_target_pairs={{1,0},{2,1},{3,2},{4,3},{5,4},{6,5},{7,6},{8,7},{9,8},{10,9},{11,1... | collective-permute-start | bytes 196616 | tf_op jit(solution)/shard_map/ppermute | solution.py:323
  57.7 5.6 %block1.1 = (bf16[256,2048]{1,0:T(8,128)(2,1)}, f32[2,128,256]{2,1,0:T(8,128)}) custom-call(s32[1]{0:T(128)} %bitcast.comp_ref, bf16[2048,256]{1,0:T(8,128)(2,1)} %get-tuple-element.17.s_ref, bf16[2,2,9,256,256]{4,3,2,1,0:T(8,128)(2,1)} %w_ref.7, f32[1,2048]{1,0:T(1,128)} %sea_ref.7), custom_call_target="tpu_custom_call" | custom-call | tf_op jit(solution)/shard_map/block1/pallas_call | solution.py:230
  63.3 0.7 %collective-permute-done.7.lo_ref = bf16[128,256]{1,0:T(8,128)(2,1)S(1)} collective-permute-done((bf16[128,256]{1,0:T(8,128)(2,1)S(1)}, bf16[128,256]{1,0:T(8,128)(2,1)S(1)}, u32[]{:S(2)}, u32[]{:S(2)}) %collective-permute-start.7) | collective-permute-done | bytes 65568 | tf_op jit(solution)/shard_map/ppermute | solution.py:322
  64.1 0.6 copy-done.8
  64.7 3.2 %finish.1 = bf16[256,2048]{1,0:T(8,128)(2,1)} custom-call(s32[1]{0:T(128)} %bitcast.comp_ref, bf16[256,2048]{1,0:T(8,128)(2,1)} %get-tuple-element.18.out_in_ref, bf16[2048,256]{1,0:T(8,128)(2,1)} %get-tuple-element.17.s_ref, f32[2,128,256]{2,1,0:T(8,128)} %get-tuple-element.19.part_ref, ...), custom_call_target="tpu_custom_call", output_to_operand_aliasing={{}: (1, {})} | custom-call | tf_op jit(solution)/shard_map/finish/pallas_call | solution.py:230
  (24 shorter events, 0.1 us)
Async XLA Ops:
  0.9 12.5 %collective-permute-start.1 = (bf16[256,128]{1,0:T(8,128)(2,1)S(1)}, bf16[256,128]{1,0:T(8,128)(2,1)S(1)}, u32[]{:S(2)}, u32[]{:S(2)}) collective-permute-start(bf16[256,128]{1,0:T(8,128)(2,1)S(1)} %get-tuple-element.21), channel_id=1, source_target_pairs={{1,0},{2,1},{3,2},{4,3},{5,4},{6,5},{7,6},{8,7},{9,8},{10,9},{11,1... | collective-permute-start | bytes 196616 | tf_op jit(solution)/shard_map/ppermute | solution.py:281
  6.4 7.0 %collective-permute-start = (bf16[256,128]{1,0:T(8,128)(2,1)S(1)}, bf16[256,128]{1,0:T(8,128)(2,1)S(1)}, u32[]{:S(2)}, u32[]{:S(2)}) collective-permute-start(bf16[256,128]{1,0:T(8,128)(2,1)S(1)} %get-tuple-element.22), channel_id=1, source_target_pairs={{0,1},{1,2},{2,3},{3,4},{4,5},{5,6},{6,7},{7,8},{8,9},{9,10},{10,1... | collective-permute-start | bytes 196616 | tf_op jit(solution)/shard_map/ppermute | solution.py:280
  13.3 23.7 %copy-start.9 = (s32[1,5,4,128]{3,2,1,0:T(4,128)S(1)}, s32[1,5,4,128]{3,2,1,0:T(4,128)}, u32[]{:S(2)}) copy-start(s32[1,5,4,128]{3,2,1,0:T(4,128)} %param.15) | copy-start | bytes 30724
  13.3 0.6 copy-start.5
  13.4 0.6 copy-start.6
  21.0 16.6 %collective-permute-start.6 = (bf16[512,128]{1,0:T(8,128)(2,1)S(1)}, bf16[512,128]{1,0:T(8,128)(2,1)S(1)}, u32[]{:S(2)}, u32[]{:S(2)}) collective-permute-start(bf16[512,128]{1,0:T(8,128)(2,1)S(1)} %get-tuple-element.23), channel_id=1, source_target_pairs={{6,0},{7,1},{8,2},{9,3},{12,6},{13,7},{14,8},{15,9},{0,10},{1,11},... | collective-permute-start | bytes 393224 | tf_op jit(solution)/shard_map/ppermute | solution.py:311
  23.0 14.7 %collective-permute-start.5 = (bf16[512,128]{1,0:T(8,128)(2,1)S(1)}, bf16[512,128]{1,0:T(8,128)(2,1)S(1)}, u32[]{:S(2)}, u32[]{:S(2)}) collective-permute-start(bf16[512,128]{1,0:T(8,128)(2,1)S(1)} %get-tuple-element.24), channel_id=1, source_target_pairs={{7,0},{8,1},{9,2},{10,3},{12,5},{13,6},{14,7},{15,8},{0,9},{1,10},... | collective-permute-start | bytes 393224 | tf_op jit(solution)/shard_map/ppermute | solution.py:311
  26.5 16.7 %collective-permute-start.4 = (bf16[512,128]{1,0:T(8,128)(2,1)S(1)}, bf16[512,128]{1,0:T(8,128)(2,1)S(1)}, u32[]{:S(2)}, u32[]{:S(2)}) collective-permute-start(bf16[512,128]{1,0:T(8,128)(2,1)S(1)} %get-tuple-element.25), channel_id=1, source_target_pairs={{8,0},{9,1},{10,2},{11,3},{12,4},{13,5},{14,6},{15,7},{0,8},{1,9},... | collective-permute-start | bytes 393224 | tf_op jit(solution)/shard_map/ppermute | solution.py:311
  29.2 15.3 %collective-permute-start.3 = (bf16[512,128]{1,0:T(8,128)(2,1)S(1)}, bf16[512,128]{1,0:T(8,128)(2,1)S(1)}, u32[]{:S(2)}, u32[]{:S(2)}) collective-permute-start(bf16[512,128]{1,0:T(8,128)(2,1)S(1)} %get-tuple-element.26), channel_id=1, source_target_pairs={{9,0},{10,1},{11,2},{13,4},{14,5},{15,6},{0,7},{1,8},{2,9},{3,10},... | collective-permute-start | bytes 393224 | tf_op jit(solution)/shard_map/ppermute | solution.py:311
  31.6 15.2 %collective-permute-start.2 = (bf16[512,128]{1,0:T(8,128)(2,1)S(1)}, bf16[512,128]{1,0:T(8,128)(2,1)S(1)}, u32[]{:S(2)}, u32[]{:S(2)}) collective-permute-start(bf16[512,128]{1,0:T(8,128)(2,1)S(1)} %get-tuple-element.27), channel_id=1, source_target_pairs={{10,0},{11,1},{14,4},{15,5},{0,6},{1,7},{2,8},{3,9},{6,12},{7,13},... | collective-permute-start | bytes 393224 | tf_op jit(solution)/shard_map/ppermute | solution.py:311
  37.6 9.1 %copy-start = (bf16[512,128]{1,0:T(8,128)(2,1)}, bf16[512,128]{1,0:T(8,128)(2,1)S(1)}, u32[]{:S(2)}) copy-start(bf16[512,128]{1,0:T(8,128)(2,1)S(1)} %collective-permute-done.6.refs_4_) | copy-start | bytes 393220
  37.7 9.1 %copy-start.1 = (bf16[512,128]{1,0:T(8,128)(2,1)}, bf16[512,128]{1,0:T(8,128)(2,1)S(1)}, u32[]{:S(2)}) copy-start(bf16[512,128]{1,0:T(8,128)(2,1)S(1)} %collective-permute-done.5.refs_3_) | copy-start | bytes 393220
  43.3 3.5 %copy-start.2 = (bf16[512,128]{1,0:T(8,128)(2,1)}, bf16[512,128]{1,0:T(8,128)(2,1)S(1)}, u32[]{:S(2)}) copy-start(bf16[512,128]{1,0:T(8,128)(2,1)S(1)} %collective-permute-done.4.refs_2_) | copy-start | bytes 393220
  44.5 2.2 %copy-start.3 = (bf16[512,128]{1,0:T(8,128)(2,1)}, bf16[512,128]{1,0:T(8,128)(2,1)S(1)}, u32[]{:S(2)}) copy-start(bf16[512,128]{1,0:T(8,128)(2,1)S(1)} %collective-permute-done.3.refs_1_) | copy-start | bytes 393220
  46.7 0.7 copy-start.4
  53.3 10.0 %collective-permute-start.8 = (bf16[128,256]{1,0:T(8,128)(2,1)S(1)}, bf16[128,256]{1,0:T(8,128)(2,1)S(1)}, u32[]{:S(2)}, u32[]{:S(2)}) collective-permute-start(bf16[128,256]{1,0:T(8,128)(2,1)S(1)} %get-tuple-element.28), channel_id=1, source_target_pairs={{1,0},{2,1},{3,2},{4,3},{5,4},{6,5},{7,6},{8,7},{9,8},{10,9},{11,1... | collective-permute-start | bytes 196616 | tf_op jit(solution)/shard_map/ppermute | solution.py:323
  57.7 6.4 %collective-permute-start.7 = (bf16[128,256]{1,0:T(8,128)(2,1)S(1)}, bf16[128,256]{1,0:T(8,128)(2,1)S(1)}, u32[]{:S(2)}, u32[]{:S(2)}) collective-permute-start(bf16[128,256]{1,0:T(8,128)(2,1)S(1)} %get-tuple-element.29), channel_id=1, source_target_pairs={{0,1},{1,2},{2,3},{3,4},{4,5},{5,6},{6,7},{7,8},{8,9},{9,10},{10,1... | collective-permute-start | bytes 196616 | tf_op jit(solution)/shard_map/ppermute | solution.py:322
  63.3 0.8 %copy-start.7 = (bf16[128,256]{1,0:T(8,128)(2,1)}, bf16[128,256]{1,0:T(8,128)(2,1)S(1)}, u32[]{:S(2)}) copy-start(bf16[128,256]{1,0:T(8,128)(2,1)S(1)} %collective-permute-done.8.hi_ref) | copy-start | bytes 196612
  64.1 0.6 copy-start.8

commit v2 on v1

v2 whole, which is shorter than its diff:
```python
import functools

import jax
import jax.numpy as jnp
from jax import lax
from jax.experimental import pallas as pl
from jax.experimental.pallas import tpu as pltpu
from jax.sharding import PartitionSpec as P

F32 = jnp.float32
BF16 = jnp.bfloat16


def dot(a, b):
    return jnp.dot(a, b, preferred_element_type=F32)


def gelu(x):
    return jax.nn.gelu(x, approximate=True)


def column(row, width):
    return jnp.broadcast_to(row, (width, row.shape[1])).T


def wet_column(comp, sea_ref, start, size):
    row = jnp.where(comp == 1, sea_ref[:, start : start + size], F32(1.0))
    col = column(row, size)
    return col


def fill_shifted(xs_ref, row, act):
    width = act.shape[0]
    at = pl.ds(row * width, width)
    xs_ref[0, at, :] = pltpu.roll(act, 1, 0).astype(BF16)
    xs_ref[1, at, :] = act.astype(BF16)
    xs_ref[2, at, :] = pltpu.roll(act, width - 1, 0).astype(BF16)


def conv_rows(xs_ref, w_ref, first, rows, width):
    acc = None
    for a in range(3):
        for b in range(3):
            part = dot(xs_ref[b, pl.ds((first + a) * width, rows * width), :], w_ref[3 * a + b])
            acc = part if acc is None else acc + part
    return acc


def zero_halo(xs_ref, rows, width):
    zeros = jnp.zeros((3, width, xs_ref.shape[2]), BF16)
    xs_ref[:, pl.ds(0, width), :] = zeros
    xs_ref[:, pl.ds((rows + 1) * width, width), :] = zeros


def wide_column(comp, sea_ref, start, size, channels):
    return jnp.concatenate([wet_column(comp, sea_ref, start, size)] * (channels // size), axis=1)


def first_block_kernel(
    comp_ref, x_ref, sea_ref, conv_hbm, state_ref, part_ref, w0_ref, w1_ref, xs_ref, sems, *, rows, width, group
):
    comp = comp_ref[0]
    channels = x_ref.shape[0]
    taps = w0_ref.shape[0]
    early = [
        pltpu.make_async_copy(conv_hbm.at[comp, 0, pl.ds(k, 1)], w0_ref.at[pl.ds(k, 1)], sems.at[k])
        for k in range(taps)
    ]
    late = pltpu.make_async_copy(conv_hbm.at[comp, 1], w1_ref, sems.at[taps])
    for copy in early:
        copy.start()
    late.start()
    zero_halo(xs_ref, rows, width)
    for r in range(rows):
        xt = x_ref[:, r * width : (r + 1) * width].astype(F32).T
        state_ref[pl.ds(r * width, width), :] = xt.astype(BF16)
        fill_shifted(xs_ref, r + 1, gelu(xt))
    for copy in early:
        copy.wait()
    for g in range(0, rows, group):
        acc = conv_rows(xs_ref, w0_ref, g, group, width)
        for r in range(g, g + group):
            piece = acc[(r - g) * width : (r - g + 1) * width]
            if r == 0:
                part_ref[0] = piece
            elif r == rows - 1:
                part_ref[1] = piece
            else:
                at = pl.ds(r * width, width)
                wet = wide_column(comp, sea_ref, r * width, width, channels)
                state_ref[at, :] = (state_ref[at, :].astype(F32) + wet * piece).astype(BF16)
    late.wait()


def pick_halo(index_row, received, own):
    width = index_row.shape[1]
    index = column(index_row.astype(F32), width)
    lane = lax.broadcasted_iota(jnp.int32, (width, width), 1).astype(F32)
    first = (index == lane).astype(F32).astype(BF16)
    second = (index == lane + width).astype(F32).astype(BF16)
    return dot(first, received) + dot(second, own)


def halo_conv(halo, w_ref, first_tap):
    width = halo.shape[0]
    return (
        dot(pltpu.roll(halo, 1, 0).astype(BF16), w_ref[first_tap])
        + dot(halo.astype(BF16), w_ref[first_tap + 1])
        + dot(pltpu.roll(halo, width - 1, 0).astype(BF16), w_ref[first_tap + 2])
    )


def gather_rows(wide, index_rows, groups):
    width = index_rows.shape[1]
    depth = wide.shape[0]
    coupling = wide.shape[1] // groups
    lane = lax.broadcasted_iota(jnp.int32, (width, width), 1).astype(F32)
    hots, picks = [], []
    for block in range(index_rows.shape[0]):
        index = column(index_rows[block : block + 1, :].astype(F32), width)
        group = jnp.floor(index * F32(1.0 / depth))
        inside = index - group * depth
        hots.append(
            jnp.concatenate(
                [(inside == lane + k * width).astype(F32).astype(BF16) for k in range(depth // width)], axis=1
            )
        )
        picks.append(group)
    taken = dot(jnp.concatenate(hots, axis=0), wide)
    group = jnp.concatenate(picks, axis=0)
    picked = taken[:, :coupling]
    for g in range(1, groups):
        picked = jnp.where(group == g, taken[:, g * coupling : (g + 1) * coupling], picked)
    return picked.astype(BF16)


def project_kernel(
    comp_ref, s_ref, part_ref, lo_ref, hi_ref, table_ref, w_ref, sea_ref, p_ref, src_ref,
    edge_ref, wide_ref, out_ref, *, rows, width, groups, slot,
):
    comp = comp_ref[0]
    channels = s_ref.shape[1]
    cells = rows * width
    weight = p_ref[comp]
    edges = []
    for side in range(2):
        r = 0 if side == 0 else rows - 1
        received = gelu((lo_ref if side == 0 else hi_ref)[...].astype(F32).T).astype(BF16)
        own_state = s_ref[pl.ds(r * width, width), :].astype(F32)
        own = gelu(own_state).astype(BF16)
        halo = pick_halo(table_ref[side : side + 1, :], received, own)
        acc = part_ref[side] + halo_conv(halo, w_ref, 6 * side)
        edge = (own_state + wide_column(comp, sea_ref, r * width, width, channels) * acc).astype(BF16)
        edge_ref[side] = edge
        edges.append(dot(edge, weight).astype(BF16))
    inner = dot(s_ref[pl.ds(width, cells - 2 * width), :], weight).astype(BF16)
    projected = jnp.concatenate([edges[0], inner, edges[1]], axis=0)
    depth = cells // groups
    wide_ref[...] = jnp.concatenate([projected[g * depth : (g + 1) * depth] for g in range(groups)], axis=1)
    out_ref[...] = gather_rows(wide_ref[...], src_ref[slot], groups)


def gather_kernel(wide_ref, src_ref, *out_refs, groups, slots):
    for slot, out_ref in zip(slots, out_refs):
        out_ref[...] = gather_rows(wide_ref[...], src_ref[slot], groups)


def land_rows(received, index_rows, depth, groups):
    width = index_rows.shape[1]
    sub = lax.broadcasted_iota(jnp.int32, (width, width), 0).astype(F32)
    sides, hots = [], []
    for block in range(index_rows.shape[0]):
        index = index_rows[block : block + 1, :].astype(F32)
        group = jnp.floor(index * F32(1.0 / depth))
        inside = index - group * depth
        values = received[block * width : (block + 1) * width, :].astype(F32)
        group_col = column(group, width)
        sides.append(
            jnp.concatenate([jnp.where(group_col == g, values, 0.0).astype(BF16) for g in range(groups)], axis=1)
        )
        hots.append(
            jnp.concatenate(
                [(inside == sub + k * width).astype(F32).astype(BF16) for k in range(depth // width)], axis=0
            )
        )
    return dot(jnp.concatenate(hots, axis=1), jnp.concatenate(sides, axis=0))


def land_first_kernel(recv_ref, dst_ref, total_ref, *, slot, groups):
    total_ref[...] = land_rows(recv_ref[...], dst_ref[slot], total_ref.shape[0], groups)


def land_more_kernel(recv_ref, dst_ref, before_ref, total_ref, *, slot, groups):
    total_ref[...] = before_ref[...] + land_rows(recv_ref[...], dst_ref[slot], total_ref.shape[0], groups)


def land_last_kernel(
    comp_ref, recv_ref, dst_ref, before_ref, s_ref, edge_ref, b_ref, state_ref, first_ref, last_ref,
    *, rows, width, groups, slot,
):
    depth = before_ref.shape[0]
    weight = b_ref[comp_ref[0]]
    coupling = weight.shape[0]
    total = before_ref[...] + land_rows(recv_ref[...], dst_ref[slot], depth, groups)
    for g in range(groups):
        remapped = total[:, g * coupling : (g + 1) * coupling].astype(BF16)
        returned = dot(remapped, weight)
        for k in range(depth // width):
            r = g * (depth // width) + k
            if r == 0:
                before = edge_ref[0]
            elif r == rows - 1:
                before = edge_ref[1]
            else:
                before = s_ref[pl.ds(r * width, width), :]
            state = (before.astype(F32) + returned[k * width : (k + 1) * width]).astype(BF16)
            state_ref[pl.ds(r * width, width), :] = state
            if r == 0:
                first_ref[...] = gelu(state.astype(F32)).astype(BF16)
            elif r == rows - 1:
                last_ref[...] = gelu(state.astype(F32)).astype(BF16)


def second_block_kernel(
    comp_ref, s_ref, w_ref, sea_ref, out_hbm, part_ref, xs_ref, out_ref, sems, *, rows, width, group
):
    comp = comp_ref[0]
    zero_halo(xs_ref, rows, width)
    for r in range(rows):
        fill_shifted(xs_ref, r + 1, gelu(s_ref[pl.ds(r * width, width), :].astype(F32)))
    copies = []
    for g in range(0, rows, group):
        acc = conv_rows(xs_ref, w_ref, g, group, width)
        for r in range(g, g + group):
            piece = acc[(r - g) * width : (r - g + 1) * width]
            if r == 0:
                part_ref[0] = piece
            elif r == rows - 1:
                part_ref[1] = piece
            else:
                row = jnp.where(comp == 1, sea_ref[:, r * width : (r + 1) * width], F32(1.0))
                state = s_ref[pl.ds(r * width, width), :].astype(F32).T
                out_ref[:, r * width : (r + 1) * width] = (state + row * piece.T).astype(BF16)
        lo = max(g, 1) * width
        at = pl.ds(lo, min(g + group, rows - 1) * width - lo)
        copy = pltpu.make_async_copy(out_ref.at[:, at], out_hbm.at[:, at], sems.at[g // group])
        copy.start()
        copies.append(copy)
    for copy in copies:
        copy.wait()


def finish_kernel(
    comp_ref, out_in, s_ref, part_ref, first_ref, last_ref, lo_ref, hi_ref, table_ref, w_ref, sea_ref,
    out_hbm, buf_ref, sems, *, rows, width,
):
    del out_in
    comp = comp_ref[0]
    copies = []
    for side in range(2):
        r = 0 if side == 0 else rows - 1
        received = (lo_ref if side == 0 else hi_ref)[...]
        own = (first_ref if side == 0 else last_ref)[...]
        halo = pick_halo(table_ref[side : side + 1, :], received, own)
        acc = part_ref[side] + halo_conv(halo, w_ref, 6 * side)
        row = jnp.where(comp == 1, sea_ref[:, r * width : (r + 1) * width], F32(1.0))
        state = s_ref[pl.ds(r * width, width), :].astype(F32).T
        buf_ref[side] = (state + row * acc.T).astype(BF16)
        copy = pltpu.make_async_copy(buf_ref.at[side], out_hbm.at[:, pl.ds(r * width, width)], sems.at[side])
        copy.start()
        copies.append(copy)
    for copy in copies:
        copy.wait()


VMEM = pl.BlockSpec(memory_space=pltpu.VMEM)
SMEM = pl.BlockSpec(memory_space=pltpu.SMEM)
HBM = pl.BlockSpec(memory_space=pl.ANY)
GRANT = 24 << 20


def call(kernel, args, specs, out_shape, out_specs=None, scratch=(), aliases=None, name=None):
    placed = [pltpu.with_memory_space_constraint(a, pltpu.VMEM) if s is VMEM else a for a, s in zip(args, specs)]
    return pl.pallas_call(
        kernel,
        in_specs=specs,
        out_specs=out_specs or [VMEM] * len(out_shape),
        out_shape=out_shape,
        scratch_shapes=scratch,
        input_output_aliases=aliases or {},
        compiler_params=pltpu.CompilerParams(vmem_limit_bytes=GRANT),
        name=name,
    )(*placed)


def on_device(
    features, conv_weight, proj_weight, back_weight, sea_fraction, halo_source, src_cells, dst_cells
):
    tile_total = lax.axis_size("tiles")
    half = tile_total // 2
    position = (lax.axis_index("tiles") + half // 2) % tile_total
    comp = (position >= half).astype(jnp.int32).reshape(1)
    _, channels, cells = features.shape
    width = halo_source.shape[-1]
    rows = cells // width
    coupling = proj_weight.shape[-1]
    slots = src_cells.shape[1]
    reach = slots // 2
    sent = src_cells.shape[2] * src_cells.shape[3]
    taps = conv_weight.shape[2]
    group, gathered, landed = 4, 4, 2

    up = [(t, (t + 1) % tile_total) for t in range(tile_total)]
    down = [(b, a) for a, b in up]

    def remap_pairs(slot):
        d = slot - reach
        pairs = [
            ((t - half - d) % tile_total, t)
            for t in range(tile_total)
            if 0 <= (t + half // 2) % tile_total % half - d < half
        ]
        idle_sources = sorted(set(range(tile_total)) - {a for a, _ in pairs})
        idle_targets = sorted(set(range(tile_total)) - {b for _, b in pairs})
        return pairs + list(zip(idle_sources, idle_targets))

    x = features[0]
    table = halo_source[0]
    src = src_cells[0]
    dst = dst_cells[0]

    lo = lax.ppermute(x[:, cells - width :], "tiles", up)
    hi = lax.ppermute(x[:, :width], "tiles", down)

    state_shape = pltpu.VMEM((cells, channels), BF16)
    part_shape = pltpu.VMEM((2, width, channels), F32)
    edge_shape = pltpu.VMEM((2, width, channels), BF16)
    row_shape = pltpu.VMEM((width, channels), BF16)
    weight_shape = pltpu.VMEM((taps, channels, channels), BF16)
    sent_shape = pltpu.VMEM((sent, coupling), BF16)
    total_shape = pltpu.VMEM((cells // landed, landed * coupling), F32)
    shifted = pltpu.VMEM((3, (rows + 2) * width, channels), BF16)

    state, part, w0, w1 = call(
        functools.partial(first_block_kernel, rows=rows, width=width, group=group),
        (comp, x, sea_fraction, conv_weight),
        [SMEM, VMEM, VMEM, HBM],
        [state_shape, part_shape, weight_shape, weight_shape],
        scratch=[shifted, pltpu.SemaphoreType.DMA((taps + 1,))],
        name="block0",
    )
    order = [reach] + [s for s in range(slots) if s != reach]
    edge, wide, middle = call(
        functools.partial(project_kernel, rows=rows, width=width, groups=gathered, slot=order[0]),
        (comp, state, part, lo, hi, table, w0, sea_fraction, proj_weight, src),
        [SMEM] + [VMEM] * 9,
        [edge_shape, pltpu.VMEM((cells // gathered, gathered * coupling), BF16), sent_shape],
        name="project",
    )
    others = call(
        functools.partial(gather_kernel, groups=gathered, slots=order[1:]),
        (wide, src),
        [VMEM] * 2,
        [sent_shape] * (slots - 1),
        name="gather",
    )
    received = [lax.ppermute(o, "tiles", remap_pairs(s)) for s, o in zip(order, [middle, *others])]
    (total,) = call(
        functools.partial(land_first_kernel, slot=order[0], groups=landed),
        (received[0], dst), [VMEM] * 2, [total_shape], name="land_first",
    )
    for k in range(1, slots - 1):
        (total,) = call(
            functools.partial(land_more_kernel, slot=order[k], groups=landed),
            (received[k], dst, total), [VMEM] * 3, [total_shape], aliases={2: 0}, name="land_more",
        )
    state, first, last = call(
        functools.partial(land_last_kernel, rows=rows, width=width, groups=landed, slot=order[-1]),
        (comp, received[-1], dst, total, state, edge, back_weight),
        [SMEM] + [VMEM] * 6,
        [state_shape, row_shape, row_shape],
        name="land_last",
    )
    lo = lax.ppermute(last, "tiles", up)
    hi = lax.ppermute(first, "tiles", down)
    out_shape = jax.ShapeDtypeStruct((channels, cells), BF16)
    out, part = call(
        functools.partial(second_block_kernel, rows=rows, width=width, group=group),
        (comp, state, w1, sea_fraction),
        [SMEM] + [VMEM] * 3,
        [out_shape, part_shape],
        out_specs=[HBM, VMEM],
        scratch=[shifted, pltpu.VMEM((channels, cells), BF16), pltpu.SemaphoreType.DMA((rows // group,))],
        name="block1",
    )
    (out,) = call(
        functools.partial(finish_kernel, rows=rows, width=width),
        (comp, out, state, part, first, last, lo, hi, table, w1, sea_fraction),
        [SMEM, HBM] + [VMEM] * 9,
        [out_shape],
        out_specs=[HBM],
        scratch=[pltpu.VMEM((2, channels, width), BF16), pltpu.SemaphoreType.DMA((2,))],
        aliases={1: 0},
        name="finish",
    )
    return out[None]


def solution(mesh):
    placed = (
        P(("runs", "tiles"), None, None),
        P(),
        P(),
        P(),
        P("tiles", None),
        P("tiles", None, None),
        P("tiles", None, None, None),
        P("tiles", None, None, None),
    )
    return jax.shard_map(
        on_device,
        mesh=mesh,
        in_specs=placed,
        out_specs=P(("runs", "tiles"), None, None),
        check_vma=False,
    )
```

time: 68.4 us -> 53 us (0.77)
  Pallas kernels: 25.3 us -> 17.8 us
  starting transfers between devices: 25.9 us -> 19.8 us
  local copies, waits for them, and re-layouts: 6.77 us -> 5.45 us
    pallas_call x5 -> x10, Pallas kernels: 25.3 us -> 17.8 us  [call(): pl.pallas_call(kernel, in_specs=specs, out_specs=out_specs or [VMEM] * le...]
    ppermute x7, starting transfers between devices: 20.4 us -> 14.3 us  [the longest x5 8.38 us: on_device(): lax.ppermute(o, 'tiles', remap_pairs(s))]
    unnamed x20 -> x18, local copies, waits for them, and re-layouts: 1.89 us -> 4.56 us
    squeeze x2 -> x0, local copies, waits for them, and re-layouts: 2.09 us -> none  [the longest x1 1.21 us: on_device(): outgoing[s]]
    another operation x2 -> x0, local copies, waits for them, and re-layouts: 1.91 us -> none  [the longest x1 1.3 us: on_device(): src = src_cells[0].reshape(-1, width)]
  transfers between devices with their start and end apart: 9 -> 9, of which waited for: 4 -> 2; matrix products, arithmetic and copies ran while one was open for 3% -> 0% of each run, Pallas kernels for 17% -> 25%
where the time goes in v2:
time: 53 us; the launch traced here: 52.7 us
  starting transfers between devices  19.8 us (37%)
  Pallas kernels  17.8 us (34%)
  waiting for transfers between devices  9.34 us (18%)
  local copies, waits for them, and re-layouts  5.45 us (10%)
    pallas_call x10, Pallas kernels, call(): pl.pallas_call(kernel, in_specs=specs, out_specs=out_specs or [VMEM] * le...  17.8 us
    ppermute x5, starting transfers between devices, on_device(): lax.ppermute(o, 'tiles', remap_pairs(s))  8.38 us
    ppermute x5, waiting for transfers between devices, on_device(): lax.ppermute(o, 'tiles', remap_pairs(s))  6.9 us
    ppermute x1, starting transfers between devices, on_device(): hi = lax.ppermute(first, 'tiles', down)  5.97 us
    ppermute x1, starting transfers between devices, on_device(): hi = lax.ppermute(x[:, :width], 'tiles', down)  5.5 us
    unnamed x18, local copies, waits for them, and re-layouts  4.56 us
    ppermute x1, waiting for transfers between devices, on_device(): lo = lax.ppermute(last, 'tiles', up)  2.43 us
  transfers between devices with their start and end apart: 9, of which 2 were waited for; matrix products, arithmetic and copies ran while one was open for 0% of the time, Pallas kernels for 25%

profile of v2, /device:TPU:0, one launch (start us, length us, event | category | flops | bytes accessed | tf_op | source)
XLA Modules:
  0.0 52.7 jit_solution(15210070774986614225)
XLA Ops:
  0.0 0.9 %fusion = (bf16[256,128]{1,0:T(8,128)(2,1)S(1)}, bf16[256,128]{1,0:T(8,128)(2,1)S(1)}) fusion(bf16[256,2048]{1,0:T(8,128)(2,1)} %bitcast.6), kind=kLoop, calls=%fused_computation | loop fusion | bytes 262144 | tf_op jit(solution)/shard_map/slice | solution.py:333
  0.9 5.5 %collective-permute-start.1 = (bf16[256,128]{1,0:T(8,128)(2,1)S(1)}, bf16[256,128]{1,0:T(8,128)(2,1)S(1)}, u32[]{:S(2)}, u32[]{:S(2)}) collective-permute-start(bf16[256,128]{1,0:T(8,128)(2,1)S(1)} %get-tuple-element.37), channel_id=1, source_target_pairs={{1,0},{2,1},{3,2},{4,3},{5,4},{6,5},{7,6},{8,7},{9,8},{10,9},{11,1... | collective-permute-start | bytes 196616 | tf_op jit(solution)/shard_map/ppermute | solution.py:333
  6.4 2.3 %copy-done = bf16[2,2,9,256,256]{4,3,2,1,0:T(8,128)(2,1)S(1)} copy-done((bf16[2,2,9,256,256]{4,3,2,1,0:T(8,128)(2,1)S(1)}, bf16[2,2,9,256,256]{4,3,2,1,0:T(8,128)(2,1)}, u32[]{:S(2)}) %copy-start) | copy-done | bytes 4718616
  8.7 1.2 %copy-done.1 = bf16[1,256,2048]{2,1,0:T(8,128)(2,1)S(1)} copy-done((bf16[1,256,2048]{2,1,0:T(8,128)(2,1)S(1)}, bf16[1,256,2048]{2,1,0:T(8,128)(2,1)}, u32[]{:S(2)}) %copy-start.1) | copy-done | bytes 1048600
  10.0 0.7 %copy-done.3 = f32[1,2048]{1,0:T(1,128)S(1)} copy-done((f32[1,2048]{1,0:T(1,128)S(1)}, f32[1,2048]{1,0:T(1,128)}, u32[]{:S(2)}) %copy-start.3) | copy-done | bytes 8216
  10.7 5.8 %block0.1 = (bf16[2048,256]{1,0:T(8,128)(2,1)S(1)}, f32[2,128,256]{2,1,0:T(8,128)S(1)}, bf16[9,256,256]{2,1,0:T(8,128)(2,1)S(1)}, bf16[9,256,256]{2,1,0:T(8,128)(2,1)S(1)}) custom-call(s32[1]{0:T(128)} %bitcast.comp_ref, bf16[256,2048]{1,0:T(8,128)(2,1)S(1)} %bitcast.7, f32[1,2048]{1,0:T(1,128)S(1)} %copy-done.3, bf16[2,2,9,256,256]{4,3,2,1,0:T(8,128)(2,1)S(1)} %copy-done), custom_call_target="tpu_custom_call" | custom-call | tf_op jit(solution)/shard_map/block0/pallas_call | solution.py:284
  16.5 1.8 %project.1 = (bf16[2,128,256]{2,1,0:T(8,128)(2,1)S(1)}, bf16[512,512]{1,0:T(8,128)(2,1)S(1)}, bf16[512,128]{1,0:T(8,128)(2,1)S(1)}) custom-call(s32[1]{0:T(128)} %bitcast.comp_ref, bf16[2048,256]{1,0:T(8,128)(2,1)S(1)} %get-tuple-element.21.s_ref, f32[2,128,256]{2,1,0:T(8,128)S(1)} %get-tuple-element.22.part_ref, ...), custom_call_target="tpu_custom_call" | custom-call | tf_op jit(solution)/shard_map/project/pallas_call | solution.py:284
  18.3 0.1 collective-permute-start.6
  18.4 1.3 %gather.1 = (bf16[512,128]{1,0:T(8,128)(2,1)S(1)}, bf16[512,128]{1,0:T(8,128)(2,1)S(1)}, bf16[512,128]{1,0:T(8,128)(2,1)S(1)}, bf16[512,128]{1,0:T(8,128)(2,1)S(1)}) custom-call(bf16[512,512]{1,0:T(8,128)(2,1)S(1)} %get-tuple-element.24.wide_ref, s32[5,4,128]{2,1,0:T(4,128)S(1)} %bitcast.14), custom_call_target="tpu_custom_call" | custom-call | tf_op jit(solution)/shard_map/gather/pallas_call | solution.py:284
  19.7 1.7 %collective-permute-start.5 = (bf16[512,128]{1,0:T(8,128)(2,1)S(1)}, bf16[512,128]{1,0:T(8,128)(2,1)S(1)}, u32[]{:S(2)}, u32[]{:S(2)}) collective-permute-start(bf16[512,128]{1,0:T(8,128)(2,1)S(1)} %get-tuple-element.28), channel_id=1, source_target_pairs={{10,0},{11,1},{14,4},{15,5},{0,6},{1,7},{2,8},{3,9},{6,12},{7,13},... | collective-permute-start | bytes 393224 | tf_op jit(solution)/shard_map/ppermute | solution.py:367
  21.4 3.2 %collective-permute-start.4 = (bf16[512,128]{1,0:T(8,128)(2,1)S(1)}, bf16[512,128]{1,0:T(8,128)(2,1)S(1)}, u32[]{:S(2)}, u32[]{:S(2)}) collective-permute-start(bf16[512,128]{1,0:T(8,128)(2,1)S(1)} %get-tuple-element.27), channel_id=1, source_target_pairs={{9,0},{10,1},{11,2},{13,4},{14,5},{15,6},{0,7},{1,8},{2,9},{3,10},... | collective-permute-start | bytes 393224 | tf_op jit(solution)/shard_map/ppermute | solution.py:367
  24.6 3.5 %collective-permute-start.2 = (bf16[512,128]{1,0:T(8,128)(2,1)S(1)}, bf16[512,128]{1,0:T(8,128)(2,1)S(1)}, u32[]{:S(2)}, u32[]{:S(2)}) collective-permute-start(bf16[512,128]{1,0:T(8,128)(2,1)S(1)} %get-tuple-element.25), channel_id=1, source_target_pairs={{6,0},{7,1},{8,2},{9,3},{12,6},{13,7},{14,8},{15,9},{0,10},{1,11},... | collective-permute-start | bytes 393224 | tf_op jit(solution)/shard_map/ppermute | solution.py:367
  28.1 0.5 %land_first.1.before_ref = f32[1024,256]{1,0:T(8,128)S(1)} custom-call(bf16[512,128]{1,0:T(8,128)(2,1)S(1)} %collective-permute-done.6.recv_ref, s32[5,4,128]{2,1,0:T(4,128)S(1)} %bitcast.8), custom_call_target="tpu_custom_call" | custom-call | tf_op jit(solution)/shard_map/land_first/pallas_call | solution.py:284
  28.6 6.9 %collective-permute-done.5.recv_ref = bf16[512,128]{1,0:T(8,128)(2,1)S(1)} collective-permute-done((bf16[512,128]{1,0:T(8,128)(2,1)S(1)}, bf16[512,128]{1,0:T(8,128)(2,1)S(1)}, u32[]{:S(2)}, u32[]{:S(2)}) %collective-permute-start.5) | collective-permute-done | bytes 131104 | tf_op jit(solution)/shard_map/ppermute | solution.py:367
  35.5 0.6 %land_more.3.before_ref = f32[1024,256]{1,0:T(8,128)S(1)} custom-call(bf16[512,128]{1,0:T(8,128)(2,1)S(1)} %collective-permute-done.5.recv_ref, s32[5,4,128]{2,1,0:T(4,128)S(1)} %bitcast.9, f32[1024,256]{1,0:T(8,128)S(1)} %land_first.1.before_ref), custom_call_target="tpu_custom_call", output_to_operand_aliasing={{}: (2, {})} | custom-call | tf_op jit(solution)/shard_map/land_more/pallas_call | solution.py:284
  36.1 0.6 %land_more.4.before_ref = f32[1024,256]{1,0:T(8,128)S(1)} custom-call(bf16[512,128]{1,0:T(8,128)(2,1)S(1)} %collective-permute-done.4.recv_ref, s32[5,4,128]{2,1,0:T(4,128)S(1)} %bitcast.10, f32[1024,256]{1,0:T(8,128)S(1)} %land_more.3.before_ref), custom_call_target="tpu_custom_call", output_to_operand_aliasing={{}: (2, {})} | custom-call | tf_op jit(solution)/shard_map/land_more/pallas_call | solution.py:284
  36.7 0.0 copy-start.6
  36.7 0.6 %land_more.5.before_ref = f32[1024,256]{1,0:T(8,128)S(1)} custom-call(bf16[512,128]{1,0:T(8,128)(2,1)S(1)} %collective-permute-done.3.recv_ref, s32[5,4,128]{2,1,0:T(4,128)S(1)} %bitcast.11, f32[1024,256]{1,0:T(8,128)S(1)} %land_more.4.before_ref), custom_call_target="tpu_custom_call", output_to_operand_aliasing={{}: (2, {})} | custom-call | tf_op jit(solution)/shard_map/land_more/pallas_call | solution.py:284
  37.3 0.3 copy-done.6
  37.6 1.2 %land_last.1 = (bf16[2048,256]{1,0:T(8,128)(2,1)S(1)}, bf16[128,256]{1,0:T(8,128)(2,1)S(1)}, bf16[128,256]{1,0:T(8,128)(2,1)S(1)}) custom-call(s32[1]{0:T(128)} %bitcast.comp_ref, bf16[512,128]{1,0:T(8,128)(2,1)S(1)} %collective-permute-done.2.recv_ref, s32[5,4,128]{2,1,0:T(4,128)S(1)} %bitcast.12, f32[1024,256]{1,0:T(8,128)S(1)} %land_more.5.before_ref, ...), custom_call_target="tpu_custom_call" | custom-call | tf_op jit(solution)/shard_map/land_last/pallas_call | solution.py:284
  38.9 6.0 %collective-permute-start.8 = (bf16[128,256]{1,0:T(8,128)(2,1)S(1)}, bf16[128,256]{1,0:T(8,128)(2,1)S(1)}, u32[]{:S(2)}, u32[]{:S(2)}) collective-permute-start(bf16[128,256]{1,0:T(8,128)(2,1)S(1)} %get-tuple-element.35.first_ref), channel_id=1, source_target_pairs={{1,0},{2,1},{3,2},{4,3},{5,4},{6,5},{7,6},{8,7},{9,8},{10,9},{11,1... | collective-permute-start | bytes 196616 | tf_op jit(solution)/shard_map/ppermute | solution.py:385
  44.8 3.9 %block1.1 = (bf16[256,2048]{1,0:T(8,128)(2,1)}, f32[2,128,256]{2,1,0:T(8,128)S(1)}) custom-call(s32[1]{0:T(128)} %bitcast.comp_ref, bf16[2048,256]{1,0:T(8,128)(2,1)S(1)} %get-tuple-element.31.s_ref, bf16[9,256,256]{2,1,0:T(8,128)(2,1)S(1)} %get-tuple-element.32.w_ref, f32[1,2048]{1,0:T(1,128)S(1)} %copy-done.4), custom_call_target="tpu_custom_call" | custom-call | tf_op jit(solution)/shard_map/block1/pallas_call | solution.py:284
  48.8 2.4 %collective-permute-done.7.lo_ref = bf16[128,256]{1,0:T(8,128)(2,1)S(1)} collective-permute-done((bf16[128,256]{1,0:T(8,128)(2,1)S(1)}, bf16[128,256]{1,0:T(8,128)(2,1)S(1)}, u32[]{:S(2)}, u32[]{:S(2)}) %collective-permute-start.7) | collective-permute-done | bytes 65568 | tf_op jit(solution)/shard_map/ppermute | solution.py:384
  51.2 1.4 %finish.1 = bf16[256,2048]{1,0:T(8,128)(2,1)} custom-call(s32[1]{0:T(128)} %bitcast.comp_ref, bf16[256,2048]{1,0:T(8,128)(2,1)} %get-tuple-element.33.out_in, bf16[2048,256]{1,0:T(8,128)(2,1)S(1)} %get-tuple-element.31.s_ref, f32[2,128,256]{2,1,0:T(8,128)S(1)} %get-tuple-element.34.part_ref, ...), custom_call_target="tpu_custom_call", output_to_operand_aliasing={{}: (1, {})} | custom-call | tf_op jit(solution)/shard_map/finish/pallas_call | solution.py:284
  (23 shorter events, 0.1 us)
Async XLA Ops:
  0.9 15.5 %collective-permute-start.1 = (bf16[256,128]{1,0:T(8,128)(2,1)S(1)}, bf16[256,128]{1,0:T(8,128)(2,1)S(1)}, u32[]{:S(2)}, u32[]{:S(2)}) collective-permute-start(bf16[256,128]{1,0:T(8,128)(2,1)S(1)} %get-tuple-element.37), channel_id=1, source_target_pairs={{1,0},{2,1},{3,2},{4,3},{5,4},{6,5},{7,6},{8,7},{9,8},{10,9},{11,1... | collective-permute-start | bytes 196616 | tf_op jit(solution)/shard_map/ppermute | solution.py:333
  6.4 10.1 %collective-permute-start = (bf16[256,128]{1,0:T(8,128)(2,1)S(1)}, bf16[256,128]{1,0:T(8,128)(2,1)S(1)}, u32[]{:S(2)}, u32[]{:S(2)}) collective-permute-start(bf16[256,128]{1,0:T(8,128)(2,1)S(1)} %get-tuple-element.38), channel_id=1, source_target_pairs={{0,1},{1,2},{2,3},{3,4},{4,5},{5,6},{6,7},{7,8},{8,9},{9,10},{10,1... | collective-permute-start | bytes 196616 | tf_op jit(solution)/shard_map/ppermute | solution.py:332
  6.4 2.3 %copy-start = (bf16[2,2,9,256,256]{4,3,2,1,0:T(8,128)(2,1)S(1)}, bf16[2,2,9,256,256]{4,3,2,1,0:T(8,128)(2,1)}, u32[]{:S(2)}) copy-start(bf16[2,2,9,256,256]{4,3,2,1,0:T(8,128)(2,1)} %conv_hbm.1) | copy-start | bytes 14155780
  8.7 1.2 %copy-start.1 = (bf16[1,256,2048]{2,1,0:T(8,128)(2,1)S(1)}, bf16[1,256,2048]{2,1,0:T(8,128)(2,1)}, u32[]{:S(2)}) copy-start(bf16[1,256,2048]{2,1,0:T(8,128)(2,1)} %param.8) | copy-start | bytes 3145732
  9.9 0.7 %copy-start.3 = (f32[1,2048]{1,0:T(1,128)S(1)}, f32[1,2048]{1,0:T(1,128)}, u32[]{:S(2)}) copy-start(f32[1,2048]{1,0:T(1,128)} %sea_ref.7) | copy-start | bytes 24580
  10.6 5.8 %copy-start.5 = (bf16[2,256,128]{2,1,0:T(8,128)(2,1)S(1)}, bf16[2,256,128]{2,1,0:T(8,128)(2,1)}, u32[]{:S(2)}) copy-start(bf16[2,256,128]{2,1,0:T(8,128)(2,1)} %p_ref.1) | copy-start | bytes 393220
  10.6 5.8 %copy-start.7 = (s32[1,5,4,128]{3,2,1,0:T(4,128)S(1)}, s32[1,5,4,128]{3,2,1,0:T(4,128)}, u32[]{:S(2)}) copy-start(s32[1,5,4,128]{3,2,1,0:T(4,128)} %param.14) | copy-start | bytes 30724
  10.7 5.8 %copy-start.8 = (s32[1,2,128]{2,1,0:T(2,128)S(1)}, s32[1,2,128]{2,1,0:T(2,128)}, u32[]{:S(2)}) copy-start(s32[1,2,128]{2,1,0:T(2,128)} %param.13) | copy-start | bytes 3076
  16.5 11.6 %copy-start.2 = (s32[1,5,4,128]{3,2,1,0:T(4,128)S(1)}, s32[1,5,4,128]{3,2,1,0:T(4,128)}, u32[]{:S(2)}) copy-start(s32[1,5,4,128]{3,2,1,0:T(4,128)} %param.15) | copy-start | bytes 30724
  18.3 9.7 %collective-permute-start.6 = (bf16[512,128]{1,0:T(8,128)(2,1)S(1)}, bf16[512,128]{1,0:T(8,128)(2,1)S(1)}, u32[]{:S(2)}, u32[]{:S(2)}) collective-permute-start(bf16[512,128]{1,0:T(8,128)(2,1)S(1)} %get-tuple-element.29), channel_id=1, source_target_pairs={{8,0},{9,1},{10,2},{11,3},{12,4},{13,5},{14,6},{15,7},{0,8},{1,9},... | collective-permute-start | bytes 393224 | tf_op jit(solution)/shard_map/ppermute | solution.py:367
  19.7 15.8 %collective-permute-start.5 = (bf16[512,128]{1,0:T(8,128)(2,1)S(1)}, bf16[512,128]{1,0:T(8,128)(2,1)S(1)}, u32[]{:S(2)}, u32[]{:S(2)}) collective-permute-start(bf16[512,128]{1,0:T(8,128)(2,1)S(1)} %get-tuple-element.28), channel_id=1, source_target_pairs={{10,0},{11,1},{14,4},{15,5},{0,6},{1,7},{2,8},{3,9},{6,12},{7,13},... | collective-permute-start | bytes 393224 | tf_op jit(solution)/shard_map/ppermute | solution.py:367
  21.4 14.7 %collective-permute-start.4 = (bf16[512,128]{1,0:T(8,128)(2,1)S(1)}, bf16[512,128]{1,0:T(8,128)(2,1)S(1)}, u32[]{:S(2)}, u32[]{:S(2)}) collective-permute-start(bf16[512,128]{1,0:T(8,128)(2,1)S(1)} %get-tuple-element.27), channel_id=1, source_target_pairs={{9,0},{10,1},{11,2},{13,4},{14,5},{15,6},{0,7},{1,8},{2,9},{3,10},... | collective-permute-start | bytes 393224 | tf_op jit(solution)/shard_map/ppermute | solution.py:367
  24.6 12.1 %collective-permute-start.3 = (bf16[512,128]{1,0:T(8,128)(2,1)S(1)}, bf16[512,128]{1,0:T(8,128)(2,1)S(1)}, u32[]{:S(2)}, u32[]{:S(2)}) collective-permute-start(bf16[512,128]{1,0:T(8,128)(2,1)S(1)} %get-tuple-element.26), channel_id=1, source_target_pairs={{7,0},{8,1},{9,2},{10,3},{12,5},{13,6},{14,7},{15,8},{0,9},{1,10},... | collective-permute-start | bytes 393224 | tf_op jit(solution)/shard_map/ppermute | solution.py:367
  24.6 12.7 %collective-permute-start.2 = (bf16[512,128]{1,0:T(8,128)(2,1)S(1)}, bf16[512,128]{1,0:T(8,128)(2,1)S(1)}, u32[]{:S(2)}, u32[]{:S(2)}) collective-permute-start(bf16[512,128]{1,0:T(8,128)(2,1)S(1)} %get-tuple-element.25), channel_id=1, source_target_pairs={{6,0},{7,1},{8,2},{9,3},{12,6},{13,7},{14,8},{15,9},{0,10},{1,11},... | collective-permute-start | bytes 393224 | tf_op jit(solution)/shard_map/ppermute | solution.py:367
  36.7 0.9 %copy-start.6 = (bf16[2,128,256]{2,1,0:T(8,128)(2,1)S(1)}, bf16[2,128,256]{2,1,0:T(8,128)(2,1)}, u32[]{:S(2)}) copy-start(bf16[2,128,256]{2,1,0:T(8,128)(2,1)} %b_ref.1) | copy-start | bytes 393220
  37.6 7.2 %copy-start.4 = (f32[1,2048]{1,0:T(1,128)S(1)}, f32[1,2048]{1,0:T(1,128)}, u32[]{:S(2)}) copy-start(f32[1,2048]{1,0:T(1,128)} %sea_ref.7) | copy-start | bytes 24580
  38.9 9.9 %collective-permute-start.8 = (bf16[128,256]{1,0:T(8,128)(2,1)S(1)}, bf16[128,256]{1,0:T(8,128)(2,1)S(1)}, u32[]{:S(2)}, u32[]{:S(2)}) collective-permute-start(bf16[128,256]{1,0:T(8,128)(2,1)S(1)} %get-tuple-element.35.first_ref), channel_id=1, source_target_pairs={{1,0},{2,1},{3,2},{4,3},{5,4},{6,5},{7,6},{8,7},{9,8},{10,9},{11,1... | collective-permute-start | bytes 196616 | tf_op jit(solution)/shard_map/ppermute | solution.py:385
  44.8 6.4 %collective-permute-start.7 = (bf16[128,256]{1,0:T(8,128)(2,1)S(1)}, bf16[128,256]{1,0:T(8,128)(2,1)S(1)}, u32[]{:S(2)}, u32[]{:S(2)}) collective-permute-start(bf16[128,256]{1,0:T(8,128)(2,1)S(1)} %get-tuple-element.36.last_ref), channel_id=1, source_target_pairs={{0,1},{1,2},{2,3},{3,4},{4,5},{5,6},{6,7},{7,8},{8,9},{9,10},{10,1... | collective-permute-start | bytes 196616 | tf_op jit(solution)/shard_map/ppermute | solution.py:384
